TPU v7x, 256 devices: a whole 4x4x8 slice. The times are simulated.
256 devices in a mesh: section: 8 (over x, y_hi), tile: 32 (over z, y_lo, core).
Axes of the slice: x: 4, y: 4 (y_hi: 2, y_lo: 2; y = y_hi * 2 + y_lo), z: 8, core: 2. Of those that a mesh axis runs over, the one named last changes fastest.
Arguments:
- carried_act: bfloat16 [8, 192, 16, 16, 256], P('section', 'tile'), may hold values from -6 to 6
- stored_out: bfloat16 [8, 192, 16, 16, 256], P('section', 'tile'), may hold values from -6 to 6
- cotangent: bfloat16 [8, 192, 16, 16, 256], P('section', 'tile'), may hold values from -6 to 6
- weights: bfloat16 [8, 2, 27, 128, 128], P('section'), may hold values from -0.109375 to 0.109375
- momentum: float32 [8, 2, 27, 128, 128], P('section'), may hold values from -6 to 6
Outputs:
- forward_out: bfloat16 [8, 192, 16, 16, 256], P('section', 'tile')
- input_grad: bfloat16 [8, 192, 16, 16, 256], P('section', 'tile')
- new_momentum: float32 [8, 2, 27, 128, 128], P('section')
All inputs are finite; a program needn't handle non-finite values.
Results may differ from a plain program's by a relative error of at most 0.006.
Values may be sent and summed in bfloat16 or wider, within the bound.
No kernel may reach another device: no remote copies, remote signals or barrier semaphores. Data moves between devices by JAX's collectives and lax.ppermute only.
A program may use at most 128 MiB of HBM per device.

v0:
```python
import functools

import jax
import jax.numpy as jnp
from jax import lax
from jax.experimental import pallas as pl
from jax.experimental.pallas import tpu as pltpu
from jax.sharding import PartitionSpec as P

momentum_decay = 0.9
grad_weight = 0.25
bf16 = jnp.bfloat16
f32 = jnp.float32
CELLS = 256
ROW = 16
TILES = 32
STEP = 288
VMEM_LIMIT = 28 << 20


def sides(layer):
    cell = lax.broadcasted_iota(jnp.int32, layer.shape, 0) % ROW
    before = jnp.where(cell == 0, 0.0, pltpu.roll(layer, 1, 0))
    after = jnp.where(cell == ROW - 1, 0.0, pltpu.roll(layer, CELLS - 1, 0))
    return before, after


def expand(wide, at, layer):
    before, after = sides(layer)
    start = pl.multiple_of(at * STEP, ROW)
    blank = jnp.zeros((ROW, 384), bf16)
    wide[pl.ds(start, ROW), :] = blank
    wide[pl.ds(start + STEP - ROW, ROW), :] = blank
    body = pl.ds(start + ROW, CELLS)
    wide[body, 0:128] = before.astype(bf16)
    wide[body, 128:256] = layer.astype(bf16)
    wide[body, 256:384] = after.astype(bf16)


def convolve(wide, at, taps):
    pieces = []
    for i in range(3):
        for j in range(3):
            start = [pl.multiple_of((at + i + h) * STEP + j * ROW, ROW) for h in range(2)]
            pieces.append(jnp.concatenate([wide[pl.ds(rows, CELLS), :] for rows in start], axis=0))
    return jnp.dot(jnp.concatenate(pieces, axis=1), taps[...], preferred_element_type=f32)


def pairs(count, body):
    def step(at, carry):
        body(at * 2)
        return carry

    lax.fori_loop(0, count // 2, step, 0)


def each(count, body):
    def step(at, carry):
        body(at)
        return carry

    lax.fori_loop(0, count, step, 0)


def half_of(value, h):
    return value[h * CELLS : h * CELLS + CELLS]


def turn(flat, at, layer):
    before, after = sides(layer)
    place = pl.ds(pl.multiple_of(at * CELLS, CELLS), CELLS)
    flat[0:128, place] = before.T.astype(bf16)
    flat[128:256, place] = layer.T.astype(bf16)
    flat[256:384, place] = after.T.astype(bf16)


def gather(to, low, mid, high, place, channel, reach):
    first = place[0] == 0
    last = place[0] == TILES - 1
    for at in range(reach):
        to[at] = jnp.where(first, 0.0, layer_of(low, low.shape[0] - reach + at, channel).astype(f32)).astype(bf16)
        to[6 + reach + at] = jnp.where(last, 0.0, layer_of(high, at, channel).astype(f32)).astype(bf16)

    def copy(at):
        to[at + reach] = layer_of(mid, at, channel)

    each(6, copy)


def outside(place, at):
    return jnp.logical_or(
        jnp.logical_and(at == 0, place[0] == 0), jnp.logical_and(at == 7, place[0] == TILES - 1)
    )


def layer_of(ref, at, low):
    return ref[at, :, :, low : low + 128].reshape(CELLS, 128)


def stored_kernel(place, z, z_low, z_high, w_g, g_out, r_out, z_wide, taps_g, ones, twos):
    taps_g[...] = w_g[0, 0].reshape(27 * 128, 128)
    gather(ones, z_low, z, z_high, place, 0, 2)
    gather(twos, z_low, z, z_high, place, 128, 1)
    each(10, lambda at: expand(z_wide, at, ones[at].astype(f32)))

    def step(at):
        g_rec = jnp.tanh(convolve(z_wide, at, taps_g))
        for h in range(2):
            part = half_of(g_rec, h)
            g_out[at + h] = 1.0 - part * part
            two = twos[at + h].astype(f32) - part
            r_out[at + h] = jnp.where(outside(place, at + h), 0.0, two).astype(bf16)

    pairs(8, step)


def turned_kernel(w, w_turned):
    def turned(tap):
        rows = pl.ds(pl.multiple_of(tap * 128, 128), 128)
        w_turned[rows, :] = w[0, 0, 26 - tap].astype(f32).T.astype(bf16)

    each(27, turned)


def inner_kernel(place, z, z_low, z_high, r, w_f, f_out, z_flat, r_flat, r_wide, taps_f, ones):
    taps_f[...] = w_f[0, 0].reshape(27 * 128, 128)
    gather(ones, z_low, z, z_high, place, 0, 1)

    def prepare(at):
        two = r[at].astype(f32)
        expand(r_wide, at, two)
        turn(r_flat, at, two)
        turn(z_flat, at, ones[at].astype(f32))

    each(8, prepare)

    def step(at):
        f_rec = jnp.tanh(convolve(r_wide, at, taps_f))
        for h in range(2):
            part = half_of(f_rec, h)
            f_out[at + h] = 1.0 - part * part

    pairs(6, step)


def gradient(place, flat, d_of, mine, other, d_pad, d_all, parts):
    blank = jnp.zeros((ROW, 128), bf16)

    def pad(at):
        start = pl.multiple_of(at * STEP, ROW)
        d_pad[pl.ds(start, ROW), :] = blank
        d_pad[pl.ds(start + STEP - ROW, ROW), :] = blank
        d_pad[pl.ds(start + ROW, CELLS), :] = d_of(at)
        rows = pl.ds(pl.multiple_of(at * CELLS, CELLS), CELLS)
        for j in range(3):
            d_all[rows, j * 128 : j * 128 + 128] = d_pad[pl.ds(start + (2 - j) * ROW, CELLS), :]

    each(6, pad)
    for i in range(3):
        part = jnp.dot(flat[:, i * CELLS : (i + 6) * CELLS], d_all[...], preferred_element_type=f32)
        for j in range(3):
            for k in range(3):
                block = part[k * 128 : k * 128 + 128, j * 128 : j * 128 + 128].astype(bf16)
                parts[9 * i + 3 * j + k] = block
    core = place[0] % 2
    deep = place[0] // 4

    def hand(m):
        near, far = 4 - m, m + 5
        for out, ahead in ((mine, jnp.where(core == 0, near, far)), (other, jnp.where(core == 0, far, near))):
            rows = pl.ds(pl.multiple_of(((deep + ahead) % 8) * 16, 16), 16)
            out[m, 0] = parts[:, rows, :]

    each(4, hand)


def grad_g_kernel(place, z_flat, pg, mine, other, d_pad, d_all, parts):
    gradient(place, z_flat, lambda at: layer_of(pg, at, 0), mine, other, d_pad, d_all, parts)


def widen(wide, low, mid, high, place, layers):
    gather(layers, low, mid, high, place, 0, 1)
    each(8, lambda at: expand(wide, at, layers[at].astype(f32)))


def first_kernel(place, pg, pg_low, pg_high, c_one, f_scale, taps, r_flat, mine_in, other_in, d_out, pf_out, mine, other, wide, d_pad, d_all, parts, layers):
    widen(wide, pg_low, pg, pg_high, place, layers)

    def step(at):
        value = convolve(wide, at, taps)
        for h in range(2):
            d_one = (layer_of(c_one, at + h, 0).astype(f32) + half_of(value, h)).astype(bf16)
            d_out[0, at + h] = d_one.reshape(16, 16, 128)
            pf_out[at + h] = (d_one.astype(f32) * f_scale[at + h]).astype(bf16).reshape(16, 16, 128)

    pairs(6, step)
    gradient(place, r_flat, lambda at: layer_of(pf_out, at, 0), mine, other, d_pad, d_all, parts)


def second_kernel(place, pf, pf_low, pf_high, c_two, taps, d_one, out, wide, layers):
    widen(wide, pf_low, pf, pf_high, place, layers)

    def step(at):
        value = convolve(wide, at, taps)
        for h in range(2):
            d_two = (layer_of(c_two, at + h, 0).astype(f32) + half_of(value, h)).astype(bf16)
            out[0, at + h] = d_two.reshape(16, 16, 128)

    pairs(6, step)


def b_one_kernel(place, a, a_low, a_high, w_f, b_out, a_wide, taps_f, ones, twos):
    taps_f[...] = w_f[0, 0].reshape(27 * 128, 128)
    gather(ones, a_low, a, a_high, place, 0, 1)
    gather(twos, a_low, a, a_high, place, 128, 2)
    each(10, lambda at: expand(a_wide, at, twos[at].astype(f32)))

    def step(at):
        f_val = jnp.tanh(convolve(a_wide, at, taps_f))
        for h in range(2):
            one = ones[at + h].astype(f32) + half_of(f_val, h)
            b_out[at + h] = jnp.where(outside(place, at + h), 0.0, one).astype(bf16)

    pairs(8, step)


def b_two_kernel(a, b, w_g, out, b_wide, taps_g):
    taps_g[...] = w_g[0, 0].reshape(27 * 128, 128)
    each(8, lambda at: expand(b_wide, at, b[at].astype(f32)))

    def step(at):
        g_val = jnp.tanh(convolve(b_wide, at, taps_g))
        for h in range(2):
            two = (layer_of(a, at + h, 128).astype(f32) + half_of(g_val, h)).astype(bf16)
            out[0, at + h, :, :, 0:128] = b[at + h + 1].reshape(16, 16, 128)
            out[0, at + h, :, :, 128:256] = two.reshape(16, 16, 128)

    pairs(6, step)


def momentum_kernel(scale, count, places, momentum, *refs):
    out = refs[-1]
    for at in range(count):

        @pl.when(pl.program_id(0) == at)
        def _():
            out[0] = momentum_decay * momentum[0] + refs[at][...].astype(f32) * scale


VMEM = pl.BlockSpec(memory_space=pltpu.VMEM)
SMEM = pl.BlockSpec(memory_space=pltpu.SMEM)


def taps_of(which):
    return pl.BlockSpec((1, 1, 27, 128, 128), lambda _: (0, which, 0, 0, 0))


def cost(layers):
    flops = layers * CELLS * 27 * 128 * 128 * 2
    return pl.CostEstimate(flops=flops, bytes_accessed=6_000_000, transcendentals=0)


def call(kernel, specs, outs, scratch, layers, out_specs=None, aliases=None):
    return pl.pallas_call(
        kernel,
        grid=(1,),
        in_specs=specs,
        out_specs=out_specs or [VMEM] * len(outs),
        out_shape=[jax.ShapeDtypeStruct(shape, kind) for shape, kind in outs],
        scratch_shapes=[pltpu.VMEM(shape, kind) for shape, kind in scratch],
        input_output_aliases=aliases or {},
        compiler_params=pltpu.CompilerParams(vmem_limit_bytes=VMEM_LIMIT),
        cost_estimate=cost(layers),
    )


def along(block, distance):
    count = lax.axis_size("section")
    return lax.ppermute(block, "section", [((i - distance) % count, i) for i in range(count)])


def halo(low_block, high_block):
    count = lax.axis_size("tile")
    low = lax.ppermute(low_block, "tile", [(i, (i + 1) % count) for i in range(count)])
    high = lax.ppermute(high_block, "tile", [((i + 1) % count, i) for i in range(count)])
    return low, high


def tiles(target):
    route = []
    for i in range(lax.axis_size("tile")):
        deep, near, core = target(i // 4, i // 2 % 2, i % 2)
        route.append((i, (deep % 8) * 4 + near * 2 + core))
    return route


def sent(block, target):
    return lax.ppermute(block, "tile", tiles(target))


def swapped(block):
    return sent(block, lambda z, y, c: (z, y, 1 - c))


def onward(block):
    return sent(block, lambda z, y, c: (z + 1 - 2 * c, y, c))


def tied(*values):
    return lax.optimization_barrier(values)


def updated(momentum, kept, chunks, places, scale):
    count = len(chunks)
    spec = pl.BlockSpec((1, 2, 27, 16, 128), lambda at, places: (0, 0, 0, places[at], 0))
    anywhere = pl.BlockSpec(memory_space=pl.ANY)
    return pl.pallas_call(
        functools.partial(momentum_kernel, scale, count),
        grid_spec=pltpu.PrefetchScalarGridSpec(
            num_scalar_prefetch=1,
            grid=(count,),
            in_specs=[spec] + [pl.BlockSpec((2, 27, 16, 128), lambda at, places: (0, 0, 0, 0))] * count + [anywhere] * len(kept),
            out_specs=spec,
        ),
        out_shape=jax.ShapeDtypeStruct(momentum.shape, f32),
        input_output_aliases={count + 2: 0} if kept else {},
        compiler_params=pltpu.CompilerParams(vmem_limit_bytes=VMEM_LIMIT),
        cost_estimate=pl.CostEstimate(flops=1_000_000, bytes_accessed=1_100_000 * count, transcendentals=0),
    )(places, momentum, *chunks, *kept)


def shards(carried_act, stored_out, cotangent, weights, momentum):
    half = 128
    field = (6, 16, 16, half)
    count = lax.axis_size("tile")
    total = stored_out.shape[1] * count * stored_out.shape[2] * stored_out.shape[3]
    scale = grad_weight / float(total) ** 0.5
    place = lax.axis_index("tile").reshape(1)
    core, deep = place[0] % 2, place[0] // 4
    wide10, wide8 = ((10 * STEP, 384), bf16), ((8 * STEP, 384), bf16)
    taps = ((27 * half, half), bf16)
    flat = ((384, 8 * CELLS), bf16)
    padded, all_d = ((6 * STEP, half), bf16), ((6 * CELLS, 384), bf16)
    eighths, parts = ((4, 2, 27, 16, half), bf16), ((27, half, half), bf16)
    ten, eight = ((10, CELLS, half), bf16), ((8, CELLS, half), bf16)
    whole = ((1, 6, 16, 16, 2 * half), bf16)
    anywhere = pl.BlockSpec(memory_space=pl.ANY)

    z = stored_out[0]
    c_two = along(cotangent[0, ..., half:], -1)
    z_low, z_high = halo(z[4:], z[:2])
    (g_turned,) = call(turned_kernel, [taps_of(1)], [taps], [], 1)(weights)
    z_low, z_high, g_turned = tied(z_low, z_high, g_turned)
    g_scale, r = call(
        stored_kernel,
        [SMEM, VMEM, VMEM, VMEM, taps_of(1)],
        [((8, CELLS, half), f32), eight],
        [wide10, taps, ten, eight],
        8,
    )(place, z, z_low, z_high, weights)
    late, r = tied(cotangent[0, ..., :half], r)
    c_one = along(late, -1)
    pg = (c_two.astype(f32) * g_scale[1:7].reshape(field)).astype(bf16)
    pg, r = tied(pg, r)
    pg_low, pg_high = halo(pg[5:], pg[:1])
    f_scale, z_flat, r_flat = call(
        inner_kernel,
        [SMEM, VMEM, VMEM, VMEM, VMEM, taps_of(0)],
        [((6, CELLS, half), f32), flat, flat],
        [wide8, taps, eight],
        6,
    )(place, z, z_low, z_high, r, weights)

    def side(which):
        return pl.BlockSpec((1, 6, 16, 16, half), lambda _: (0, 0, 0, 0, which))

    def part(which):
        return pl.BlockSpec((4, 1, 27, 16, half), lambda _: (0, which, 0, 0, 0))

    mine, other = call(
        grad_g_kernel, [SMEM, VMEM, VMEM], [eighths] * 2, [padded, all_d, parts], 6, [part(1), part(1)]
    )(place, z_flat, pg)
    act, pg_low, pg_high = tied(carried_act[0], pg_low, pg_high)
    a = along(act, 1)
    d_one, pf, mine, other = call(
        first_kernel,
        [SMEM] + [VMEM] * 7 + [anywhere] * 2,
        [whole, (field, bf16), eighths, eighths],
        [wide8, padded, all_d, parts, eight],
        12,
        [side(0), VMEM, part(0), part(0)],
        {8: 2, 9: 3},
    )(place, pg, pg_low, pg_high, c_one, f_scale, g_turned, r_flat, mine, other)

    from_core = swapped(other)
    from_core, weights_later = tied(from_core, weights)
    pf_low, pf_high = halo(pf[5:], pf[:1])

    def own(m):
        return mine[m].astype(f32) + from_core[m].astype(f32)

    sign = jnp.where(core == 0, 7, 1)
    steps = jnp.stack([0 * sign, sign, -sign, 2 * sign, -2 * sign, 3 * sign, -3 * sign, 4 * sign])
    places = (deep + steps + 32) % 8
    got = onward(own(0).astype(bf16))
    (f_turned,) = call(turned_kernel, [taps_of(0)], [taps], [], 1)(weights_later)
    got, places, f_turned, pf_low, pf_high = tied(got, places, f_turned, pf_low, pf_high)
    got = onward((own(1) + got.astype(f32)).astype(bf16))
    got = onward((own(2) + got.astype(f32)).astype(bf16))
    got, a = tied(got, a)
    a_low, a_high = halo(a[4:], a[:2])
    held = (own(3) + got.astype(f32)).astype(bf16)
    straight = sent(held, lambda z, y, c: (z + 1 - c, y, c))
    across = sent(held, lambda z, y, c: (z + 1 - c, 1 - y, c))
    held = (straight.astype(f32) + across.astype(f32)).astype(bf16)
    held = (held.astype(f32) + swapped(held).astype(f32)).astype(bf16)
    first = onward(held)
    (out_grad,) = call(
        second_kernel, [SMEM] + [VMEM] * 5 + [anywhere], [whole], [wide8, eight], 6, [side(1)], {6: 0}
    )(place, pf, pf_low, pf_high, c_two, f_turned, d_one)
    first, a_low, a_high, out_grad = tied(first, a_low, a_high, out_grad)
    second = onward(first)
    first_other = swapped(first)
    (b_one,) = call(
        b_one_kernel, [SMEM, VMEM, VMEM, VMEM, taps_of(0)], [eight], [wide10, taps, eight, ten], 8
    )(place, a, a_low, a_high, weights)
    second, first_other, b_one = tied(second, first_other, b_one)
    third = onward(second)
    second_other = swapped(second)
    (out_fwd,) = call(b_two_kernel, [VMEM, VMEM, taps_of(1)], [whole], [wide8, taps], 6)(a, b_one, weights)
    third, second_other, out_fwd = tied(third, second_other, out_fwd)
    fourth = onward(third)
    third_other = swapped(third)
    new = updated(momentum, [], [held, first, first_other, second, second_other], places[:5], scale)
    fourth, third_other, new = tied(fourth, third_other, new)
    new = updated(momentum, [new], [third, third_other, fourth], places[5:], scale)
    return (out_fwd, out_grad, new)


def solution(mesh):
    placed = (
        P("section", "tile", None, None, None),
        P("section", "tile", None, None, None),
        P("section", "tile", None, None, None),
        P("section", None, None, None, None),
        P("section", None, None, None, None),
    )
    return jax.shard_map(
        shards,
        mesh=mesh,
        in_specs=placed,
        out_specs=(
            P("section", "tile", None, None, None),
            P("section", "tile", None, None, None),
            P("section", None, None, None, None),
        ),
        check_vma=False,
    )
```

profile of v0, /device:TPU:8, one launch (start us, length us, event | category | flops | bytes accessed | tf_op | source)
XLA Modules:
  0.0 121.9 jit_solution(10776426223322587957)
XLA Ops:
  0.7 2.0 %slice_bitcast_fusion.2 = (bf16[2,16,16,256]{3,2,1,0:T(8,128)(2,1)}, bf16[2,16,16,256]{3,2,1,0:T(8,128)(2,1)}) fusion(bf16[1,6,16,16,256]{4,3,2,1,0:T(8,128)(2,1)} %param.6), kind=kLoop, calls=%fused_computation.12 | loop fusion | bytes 1048576 | tf_op jit(solution)/shard_map/slice | solution.py:351
  2.6 1.7 %collective-permute-start.2 = (bf16[2,16,16,256]{3,2,1,0:T(8,128)(2,1)}, bf16[2,16,16,256]{3,2,1,0:T(8,128)(2,1)}, u32[]{:S(2)}, u32[]{:S(2)}) collective-permute-start(bf16[2,16,16,256]{3,2,1,0:T(8,128)(2,1)} %get-tuple-element.93), channel_id=1, source_target_pairs={{1,0},{2,1},{3,2},{4,3},{5,4},{6,5},{7,6},{8,7},{9,8},{10,9},{11,1... | collective-permute-start | bytes 786440 | tf_op jit(solution)/shard_map/ppermute | solution.py:285
  4.4 2.1 %slice_bitcast_fusion = (bf16[6,16,16,128]{3,2,1,0:T(8,128)(2,1)}, bf16[6,16,16,128]{3,2,1,0:T(8,128)(2,1)}) fusion(bf16[1,6,16,16,256]{4,3,2,1,0:T(8,128)(2,1)} %param.7), kind=kLoop, calls=%fused_computation.10 | loop fusion | bytes 1572864 | tf_op jit(solution)/shard_map/squeeze | solution.py:361
  6.5 4.5 %collective-permute-start = (bf16[6,16,16,128]{3,2,1,0:T(8,128)(2,1)}, bf16[6,16,16,128]{3,2,1,0:T(8,128)(2,1)S(1)}, u32[]{:S(2)}, u32[]{:S(2)}) collective-permute-start(bf16[6,16,16,128]{3,2,1,0:T(8,128)(2,1)} %get-tuple-element.92), channel_id=1, source_target_pairs={{32,0},{64,32},{96,64},{128,96},{160,128},{192,160},{224,192},{0,2... | collective-permute-start | bytes 1179656 | tf_op jit(solution)/shard_map/ppermute | solution.py:279
  11.0 2.7 %shard_map.76.taps = bf16[3456,128]{1,0:T(8,128)(2,1)S(1)} custom-call(bf16[1,2,27,128,128]{4,3,2,1,0:T(8,128)(2,1)S(1)} %copy-done.1), custom_call_target="tpu_custom_call" | custom-call | flops 226492416 | bytes 6000000 | tf_op jit(solution)/shard_map/pallas_call | solution.py:352
  13.8 6.4 %shard_map.77 = (f32[8,256,128]{2,1,0:T(8,128)S(1)}, bf16[8,256,128]{2,1,0:T(8,128)(2,1)S(1)}) custom-call(s32[1]{0:T(128)} %bitcast.place, bf16[6,16,16,256]{3,2,1,0:T(8,128)(2,1)S(1)} %bitcast.34, bf16[2,16,16,256]{3,2,1,0:T(8,128)(2,1)S(1)} %collective-permute-done.1.z_low, bf16[2,16,16,256]{3,2,1,0:T(8,128)(2,1)} %collective-permute-done.2.z_high, ...), custom_call_target="tpu_custom_call" | custom-call | flops 1811939328 | bytes 6000000 | tf_op jit(solution)/shard_map/pallas_call | solution.py:354
  20.2 1.3 %collective-permute-start.5 = (bf16[6,16,16,128]{3,2,1,0:T(8,128)(2,1)S(1)}, bf16[6,16,16,128]{3,2,1,0:T(8,128)(2,1)S(1)}, u32[]{:S(2)}, u32[]{:S(2)}) collective-permute-start(bf16[6,16,16,128]{3,2,1,0:T(8,128)(2,1)S(1)} %copy-done.3), channel_id=1, source_target_pairs={{32,0},{64,32},{96,64},{128,96},{160,128},{192,160},{224,192},{0,2... | collective-permute-start | bytes 1179656 | tf_op jit(solution)/shard_map/ppermute | solution.py:279
  22.9 5.9 %collective-permute-start.4 = (bf16[1,16,16,128]{3,2,1,0:T(8,128)(2,1)S(1)}, bf16[1,16,16,128]{3,2,1,0:T(8,128)(2,1)S(1)}, u32[]{:S(2)}, u32[]{:S(2)}) collective-permute-start(bf16[1,16,16,128]{3,2,1,0:T(8,128)(2,1)S(1)} %get-tuple-element.97), channel_id=1, source_target_pairs={{1,0},{2,1},{3,2},{4,3},{5,4},{6,5},{7,6},{8,7},{9,8},{10,9},{11,1... | collective-permute-start | bytes 196616 | tf_op jit(solution)/shard_map/ppermute | solution.py:285
  28.7 6.0 %shard_map.78 = (f32[6,256,128]{2,1,0:T(8,128)S(1)}, bf16[384,2048]{1,0:T(8,128)(2,1)S(1)}, bf16[384,2048]{1,0:T(8,128)(2,1)S(1)}) custom-call(s32[1]{0:T(128)} %bitcast.place, bf16[6,16,16,256]{3,2,1,0:T(8,128)(2,1)S(1)} %bitcast.35, bf16[2,16,16,256]{3,2,1,0:T(8,128)(2,1)S(1)} %collective-permute-done.1.z_low, ...), custom_call_target="tpu_custom_call" | custom-call | flops 1358954496 | bytes 6000000 | tf_op jit(solution)/shard_map/pallas_call | solution.py:366
  34.7 3.2 %shard_map.79 = (bf16[4,2,27,16,128]{4,3,2,1,0:T(8,128)(2,1)S(1)}, bf16[4,2,27,16,128]{4,3,2,1,0:T(8,128)(2,1)}) custom-call(s32[1]{0:T(128)} %bitcast.place, bf16[384,2048]{1,0:T(8,128)(2,1)S(1)} %get-tuple-element.59.z_flat, bf16[6,16,16,128]{3,2,1,0:T(8,128)(2,1)S(1)} %multiply_convert_fusion.pg), custom_call_target="tpu_custom_call" | custom-call | flops 1358954496 | bytes 6000000 | tf_op jit(solution)/shard_map/pallas_call | solution.py:380
  38.0 7.2 %shard_map.80 = (bf16[1,6,16,16,256]{4,3,2,1,0:T(8,128)(2,1)}, bf16[6,16,16,128]{3,2,1,0:T(8,128)(2,1)S(1)}, bf16[4,2,27,16,128]{4,3,2,1,0:T(8,128)(2,1)S(1)}, bf16[4,2,27,16,128]{4,3,2,1,0:T(8,128)(2,1)}) custom-call(s32[1]{0:T(128)} %bitcast.place, ...), custom_call_target="tpu_custom_call", output_to_operand_aliasing={{2}: (8, {}), {3}: (9, {})} | custom-call | flops 2717908992 | bytes 6000000 | tf_op jit(solution)/shard_map/pallas_call | solution.py:385
  45.8 1.7 %collective-permute-start.9 = (bf16[1,16,16,128]{3,2,1,0:T(8,128)(2,1)S(1)}, bf16[1,16,16,128]{3,2,1,0:T(8,128)(2,1)S(1)}, u32[]{:S(2)}, u32[]{:S(2)}) collective-permute-start(bf16[1,16,16,128]{3,2,1,0:T(8,128)(2,1)S(1)} %get-tuple-element.95), channel_id=1, source_target_pairs={{1,0},{2,1},{3,2},{4,3},{5,4},{6,5},{7,6},{8,7},{9,8},{10,9},{11,1... | collective-permute-start | bytes 196616 | tf_op jit(solution)/shard_map/ppermute | solution.py:285
  49.0 2.7 %collective-permute-start.12 = (bf16[6,16,16,256]{3,2,1,0:T(8,128)(2,1)}, bf16[6,16,16,256]{3,2,1,0:T(8,128)(2,1)S(1)}, u32[]{:S(2)}, u32[]{:S(2)}) collective-permute-start(bf16[6,16,16,256]{3,2,1,0:T(8,128)(2,1)} %bitcast.38), channel_id=1, source_target_pairs={{224,0},{0,32},{32,64},{64,96},{96,128},{128,160},{160,192},{192,2... | collective-permute-start | bytes 2359304 | tf_op jit(solution)/shard_map/ppermute | solution.py:279
  51.7 2.7 %shard_map.81.taps = bf16[3456,128]{1,0:T(8,128)(2,1)S(1)} custom-call(bf16[1,2,27,128,128]{4,3,2,1,0:T(8,128)(2,1)S(1)} %copy-done.1), custom_call_target="tpu_custom_call" | custom-call | flops 226492416 | bytes 6000000 | tf_op jit(solution)/shard_map/pallas_call | solution.py:406
  54.5 3.3 %collective-permute-done.7 = bf16[2,27,16,128]{3,2,1,0:T(8,128)(2,1)S(1)} collective-permute-done((bf16[2,27,16,128]{3,2,1,0:T(8,128)(2,1)S(1)}, bf16[2,27,16,128]{3,2,1,0:T(8,128)(2,1)S(1)}, u32[]{:S(2)}, u32[]{:S(2)}) %collective-permute-start.7) | collective-permute-done | bytes 221216 | tf_op jit(solution)/shard_map/ppermute | solution.py:298
  58.9 7.1 %collective-permute-done.10 = bf16[2,27,16,128]{3,2,1,0:T(8,128)(2,1)S(1)} collective-permute-done((bf16[2,27,16,128]{3,2,1,0:T(8,128)(2,1)S(1)}, bf16[2,27,16,128]{3,2,1,0:T(8,128)(2,1)S(1)}, u32[]{:S(2)}, u32[]{:S(2)}) %collective-permute-start.10) | collective-permute-done | bytes 221216 | tf_op jit(solution)/shard_map/ppermute | solution.py:298
  67.1 2.5 %collective-permute-done.12.a = bf16[6,16,16,256]{3,2,1,0:T(8,128)(2,1)S(1)} collective-permute-done((bf16[6,16,16,256]{3,2,1,0:T(8,128)(2,1)}, bf16[6,16,16,256]{3,2,1,0:T(8,128)(2,1)S(1)}, u32[]{:S(2)}, u32[]{:S(2)}) %collective-permute-start.12) | collective-permute-done | bytes 786464 | tf_op jit(solution)/shard_map/ppermute | solution.py:279
  69.6 4.6 %collective-permute-done.11 = bf16[2,27,16,128]{3,2,1,0:T(8,128)(2,1)S(1)} collective-permute-done((bf16[2,27,16,128]{3,2,1,0:T(8,128)(2,1)S(1)}, bf16[2,27,16,128]{3,2,1,0:T(8,128)(2,1)S(1)}, u32[]{:S(2)}, u32[]{:S(2)}) %collective-permute-start.11) | collective-permute-done | bytes 221216 | tf_op jit(solution)/shard_map/ppermute | solution.py:298
  76.1 3.9 %collective-permute-start.13 = (bf16[2,27,16,128]{3,2,1,0:T(8,128)(2,1)S(1)}, bf16[2,27,16,128]{3,2,1,0:T(8,128)(2,1)S(1)}, u32[]{:S(2)}, u32[]{:S(2)}) collective-permute-start(bf16[2,27,16,128]{3,2,1,0:T(8,128)(2,1)S(1)} %fusion.2), channel_id=1, source_target_pairs={{0,4},{1,1},{2,6},{3,3},{4,8},{5,5},{6,10},{7,7},{8,12},{9,9},{10,... | collective-permute-start | bytes 663560 | tf_op jit(solution)/shard_map/ppermute | solution.py:298
  80.0 3.5 %collective-permute-done.14 = bf16[2,27,16,128]{3,2,1,0:T(8,128)(2,1)S(1)} collective-permute-done((bf16[2,27,16,128]{3,2,1,0:T(8,128)(2,1)S(1)}, bf16[2,27,16,128]{3,2,1,0:T(8,128)(2,1)S(1)}, u32[]{:S(2)}, u32[]{:S(2)}) %collective-permute-start.14) | collective-permute-done | bytes 221216 | tf_op jit(solution)/shard_map/ppermute | solution.py:298
  83.5 4.2 %collective-permute-done.13 = bf16[2,27,16,128]{3,2,1,0:T(8,128)(2,1)S(1)} collective-permute-done((bf16[2,27,16,128]{3,2,1,0:T(8,128)(2,1)S(1)}, bf16[2,27,16,128]{3,2,1,0:T(8,128)(2,1)S(1)}, u32[]{:S(2)}, u32[]{:S(2)}) %collective-permute-start.13) | collective-permute-done | bytes 221216 | tf_op jit(solution)/shard_map/ppermute | solution.py:298
  88.5 1.3 %collective-permute-start.18 = (bf16[2,16,16,256]{3,2,1,0:T(8,128)(2,1)S(1)}, bf16[2,16,16,256]{3,2,1,0:T(8,128)(2,1)S(1)}, u32[]{:S(2)}, u32[]{:S(2)}) collective-permute-start(bf16[2,16,16,256]{3,2,1,0:T(8,128)(2,1)S(1)} %get-tuple-element.89), channel_id=1, source_target_pairs={{1,0},{2,1},{3,2},{4,3},{5,4},{6,5},{7,6},{8,7},{9,8},{10,9},{11,1... | collective-permute-start | bytes 786440 | tf_op jit(solution)/shard_map/ppermute | solution.py:285
  89.9 4.6 %shard_map.82 = bf16[1,6,16,16,256]{4,3,2,1,0:T(8,128)(2,1)} custom-call(s32[1]{0:T(128)} %bitcast.place, bf16[6,16,16,128]{3,2,1,0:T(8,128)(2,1)S(1)} %get-tuple-element.66.pf, bf16[1,16,16,128]{3,2,1,0:T(8,128)(2,1)S(1)} %collective-permute-done.8.pf_low, ...), custom_call_target="tpu_custom_call", output_to_operand_aliasing={{}: (6, {})} | custom-call | flops 1358954496 | bytes 6000000 | tf_op jit(solution)/shard_map/pallas_call | solution.py:418
  94.9 1.4 %collective-permute-done.18.a_high = bf16[2,16,16,256]{3,2,1,0:T(8,128)(2,1)S(1)} collective-permute-done((bf16[2,16,16,256]{3,2,1,0:T(8,128)(2,1)S(1)}, bf16[2,16,16,256]{3,2,1,0:T(8,128)(2,1)S(1)}, u32[]{:S(2)}, u32[]{:S(2)}) %collective-permute-start.18) | collective-permute-done | bytes 262176 | tf_op jit(solution)/shard_map/ppermute | solution.py:285
  97.0 2.8 %collective-permute-start.20 = (bf16[2,27,16,128]{3,2,1,0:T(8,128)(2,1)S(1)}, bf16[2,27,16,128]{3,2,1,0:T(8,128)(2,1)S(1)}, u32[]{:S(2)}, u32[]{:S(2)}) collective-permute-start(bf16[2,27,16,128]{3,2,1,0:T(8,128)(2,1)S(1)} %collective-permute-done.16.refs_1_), channel_id=1, source_target_pairs={{0,1},{1,0},{2,3},{3,2},{4,5},{5,4},{6,7},{7,6},{8,9},{9,8},{10,11... | collective-permute-start | bytes 663560 | tf_op jit(solution)/shard_map/ppermute | solution.py:298
  99.8 5.4 %shard_map.83.b = bf16[8,256,128]{2,1,0:T(8,128)(2,1)S(1)} custom-call(s32[1]{0:T(128)} %bitcast.place, bf16[6,16,16,256]{3,2,1,0:T(8,128)(2,1)S(1)} %collective-permute-done.12.a, bf16[2,16,16,256]{3,2,1,0:T(8,128)(2,1)S(1)} %collective-permute-done.17.a_low, bf16[2,16,16,256]{3,2,1,0:T(8,128)(2,1)S(1)} %collective-permute-done.18.a_high, ...), custom_call_target="tpu_custom_call" | custom-call | flops 1811939328 | bytes 6000000 | tf_op jit(solution)/shard_map/pallas_call | solution.py:424
  106.0 4.7 %shard_map.84 = bf16[1,6,16,16,256]{4,3,2,1,0:T(8,128)(2,1)} custom-call(bf16[6,16,16,256]{3,2,1,0:T(8,128)(2,1)S(1)} %collective-permute-done.12.a, bf16[8,256,128]{2,1,0:T(8,128)(2,1)S(1)} %shard_map.83.b, bf16[1,2,27,128,128]{4,3,2,1,0:T(8,128)(2,1)S(1)} %copy-done.1), custom_call_target="tpu_custom_call" | custom-call | flops 1358954496 | bytes 6000000 | tf_op jit(solution)/shard_map/pallas_call | solution.py:430
  110.7 1.7 %collective-permute-done.21.refs_0_ = bf16[2,27,16,128]{3,2,1,0:T(8,128)(2,1)S(1)} collective-permute-done((bf16[2,27,16,128]{3,2,1,0:T(8,128)(2,1)S(1)}, bf16[2,27,16,128]{3,2,1,0:T(8,128)(2,1)S(1)}, u32[]{:S(2)}, u32[]{:S(2)}) %collective-permute-start.21) | collective-permute-done | bytes 221216 | tf_op jit(solution)/shard_map/ppermute | solution.py:298
  112.4 1.1 collective-permute-start.24
  113.6 3.2 %shard_map.85.refs_3_ = f32[1,2,27,128,128]{4,3,2,1,0:T(8,128)} custom-call(s32[5]{0:T(128)S(1)} %bitcast.36, f32[1,2,27,128,128]{4,3,2,1,0:T(8,128)S(1)} %copy-done, bf16[2,27,16,128]{3,2,1,0:T(8,128)(2,1)S(1)} %add_convert_fusion.refs_0_, bf16[2,27,16,128]{3,2,1,0:T(8,128)(2,1)S(1)} %collective-permute-done.16.refs_1_, ...), custom_call_target="tpu_custom_call" | custom-call | flops 1000000 | bytes 5500000 | tf_op jit(solution)/shard_map/pallas_call | solution.py:317
  116.8 2.8 %collective-permute-done.23.refs_2_ = bf16[2,27,16,128]{3,2,1,0:T(8,128)(2,1)S(1)} collective-permute-done((bf16[2,27,16,128]{3,2,1,0:T(8,128)(2,1)S(1)}, bf16[2,27,16,128]{3,2,1,0:T(8,128)(2,1)S(1)}, u32[]{:S(2)}, u32[]{:S(2)}) %collective-permute-start.23) | collective-permute-done | bytes 221216 | tf_op jit(solution)/shard_map/ppermute | solution.py:298
  119.6 2.3 %shard_map.86 = f32[1,2,27,128,128]{4,3,2,1,0:T(8,128)} custom-call(s32[3]{0:T(128)S(1)} %slice.90.places, f32[1,2,27,128,128]{4,3,2,1,0:T(8,128)S(1)} %copy-done, bf16[2,27,16,128]{3,2,1,0:T(8,128)(2,1)S(1)} %collective-permute-done.21.refs_0_, bf16[2,27,16,128]{3,2,1,0:T(8,128)(2,1)S(1)} %collective-permute-done.24.refs_1_, ...), custom_call_target="tpu_custom_call", output_to_operand_aliasing={{}: (5, {})} | custom-call | flops 1000000 | bytes 3300000 | tf_op jit(solution)/shard_map/pallas_call | solution.py:317
  (53 shorter events, 10.5 us)
Async XLA Ops:
  0.6 13.2 %copy-start.2 = (bf16[1,6,16,16,256]{4,3,2,1,0:T(8,128)(2,1)S(1)}, bf16[1,6,16,16,256]{4,3,2,1,0:T(8,128)(2,1)}, u32[]{:S(2)}) copy-start(bf16[1,6,16,16,256]{4,3,2,1,0:T(8,128)(2,1)} %param.6) | copy-start | bytes 2359300
  0.6 10.4 %copy-start.1 = (bf16[1,2,27,128,128]{4,3,2,1,0:T(8,128)(2,1)S(1)}, bf16[1,2,27,128,128]{4,3,2,1,0:T(8,128)(2,1)}, u32[]{:S(2)}) copy-start(bf16[1,2,27,128,128]{4,3,2,1,0:T(8,128)(2,1)} %w_g.3) | copy-start | bytes 5308420
  2.6 11.1 %collective-permute-start.1 = (bf16[2,16,16,256]{3,2,1,0:T(8,128)(2,1)}, bf16[2,16,16,256]{3,2,1,0:T(8,128)(2,1)S(1)}, u32[]{:S(2)}, u32[]{:S(2)}) collective-permute-start(bf16[2,16,16,256]{3,2,1,0:T(8,128)(2,1)} %get-tuple-element.94), channel_id=1, source_target_pairs={{0,1},{1,2},{2,3},{3,4},{4,5},{5,6},{6,7},{7,8},{8,9},{9,10},{10,1... | collective-permute-start | bytes 786440 | tf_op jit(solution)/shard_map/ppermute | solution.py:284
  2.6 11.1 %collective-permute-start.2 = (bf16[2,16,16,256]{3,2,1,0:T(8,128)(2,1)}, bf16[2,16,16,256]{3,2,1,0:T(8,128)(2,1)}, u32[]{:S(2)}, u32[]{:S(2)}) collective-permute-start(bf16[2,16,16,256]{3,2,1,0:T(8,128)(2,1)} %get-tuple-element.93), channel_id=1, source_target_pairs={{1,0},{2,1},{3,2},{4,3},{5,4},{6,5},{7,6},{8,7},{9,8},{10,9},{11,1... | collective-permute-start | bytes 786440 | tf_op jit(solution)/shard_map/ppermute | solution.py:285
  6.5 16.0 %collective-permute-start = (bf16[6,16,16,128]{3,2,1,0:T(8,128)(2,1)}, bf16[6,16,16,128]{3,2,1,0:T(8,128)(2,1)S(1)}, u32[]{:S(2)}, u32[]{:S(2)}) collective-permute-start(bf16[6,16,16,128]{3,2,1,0:T(8,128)(2,1)} %get-tuple-element.92), channel_id=1, source_target_pairs={{32,0},{64,32},{96,64},{128,96},{160,128},{192,160},{224,192},{0,2... | collective-permute-start | bytes 1179656 | tf_op jit(solution)/shard_map/ppermute | solution.py:279
  13.8 6.4 %copy-start.3 = (bf16[6,16,16,128]{3,2,1,0:T(8,128)(2,1)S(1)}, bf16[6,16,16,128]{3,2,1,0:T(8,128)(2,1)}, u32[]{:S(2)}) copy-start(bf16[6,16,16,128]{3,2,1,0:T(8,128)(2,1)} %get-tuple-element.54) | copy-start | bytes 1179652
  20.2 17.7 %collective-permute-start.5 = (bf16[6,16,16,128]{3,2,1,0:T(8,128)(2,1)S(1)}, bf16[6,16,16,128]{3,2,1,0:T(8,128)(2,1)S(1)}, u32[]{:S(2)}, u32[]{:S(2)}) collective-permute-start(bf16[6,16,16,128]{3,2,1,0:T(8,128)(2,1)S(1)} %copy-done.3), channel_id=1, source_target_pairs={{32,0},{64,32},{96,64},{128,96},{160,128},{192,160},{224,192},{0,2... | collective-permute-start | bytes 1179656 | tf_op jit(solution)/shard_map/ppermute | solution.py:279
  22.6 15.4 %collective-permute-start.3 = (bf16[1,16,16,128]{3,2,1,0:T(8,128)(2,1)S(1)}, bf16[1,16,16,128]{3,2,1,0:T(8,128)(2,1)S(1)}, u32[]{:S(2)}, u32[]{:S(2)}) collective-permute-start(bf16[1,16,16,128]{3,2,1,0:T(8,128)(2,1)S(1)} %get-tuple-element.98), channel_id=1, source_target_pairs={{0,1},{1,2},{2,3},{3,4},{4,5},{5,6},{6,7},{7,8},{8,9},{9,10},{10,1... | collective-permute-start | bytes 196616 | tf_op jit(solution)/shard_map/ppermute | solution.py:284
  22.9 15.1 %collective-permute-start.4 = (bf16[1,16,16,128]{3,2,1,0:T(8,128)(2,1)S(1)}, bf16[1,16,16,128]{3,2,1,0:T(8,128)(2,1)S(1)}, u32[]{:S(2)}, u32[]{:S(2)}) collective-permute-start(bf16[1,16,16,128]{3,2,1,0:T(8,128)(2,1)S(1)} %get-tuple-element.97), channel_id=1, source_target_pairs={{1,0},{2,1},{3,2},{4,3},{5,4},{6,5},{7,6},{8,7},{9,8},{10,9},{11,1... | collective-permute-start | bytes 196616 | tf_op jit(solution)/shard_map/ppermute | solution.py:285
  45.1 2.8 %collective-permute-start.6 = (bf16[4,2,27,16,128]{4,3,2,1,0:T(8,128)(2,1)}, bf16[4,2,27,16,128]{4,3,2,1,0:T(8,128)(2,1)}, u32[]{:S(2)}, u32[]{:S(2)}) collective-permute-start(bf16[4,2,27,16,128]{4,3,2,1,0:T(8,128)(2,1)} %get-tuple-element.63), channel_id=1, source_target_pairs={{0,1},{1,0},{2,3},{3,2},{4,5},{5,4},{6,7},{7,6},{8,9},{9,8},{10,11... | collective-permute-start | bytes 2654216 | tf_op jit(solution)/shard_map/ppermute | solution.py:298
  45.2 9.2 %collective-permute-start.8 = (bf16[1,16,16,128]{3,2,1,0:T(8,128)(2,1)S(1)}, bf16[1,16,16,128]{3,2,1,0:T(8,128)(2,1)S(1)}, u32[]{:S(2)}, u32[]{:S(2)}) collective-permute-start(bf16[1,16,16,128]{3,2,1,0:T(8,128)(2,1)S(1)} %get-tuple-element.96), channel_id=1, source_target_pairs={{0,1},{1,2},{2,3},{3,4},{4,5},{5,6},{6,7},{7,8},{8,9},{9,10},{10,1... | collective-permute-start | bytes 196616 | tf_op jit(solution)/shard_map/ppermute | solution.py:284
  45.8 8.6 %collective-permute-start.9 = (bf16[1,16,16,128]{3,2,1,0:T(8,128)(2,1)S(1)}, bf16[1,16,16,128]{3,2,1,0:T(8,128)(2,1)S(1)}, u32[]{:S(2)}, u32[]{:S(2)}) collective-permute-start(bf16[1,16,16,128]{3,2,1,0:T(8,128)(2,1)S(1)} %get-tuple-element.95), channel_id=1, source_target_pairs={{1,0},{2,1},{3,2},{4,3},{5,4},{6,5},{7,6},{8,7},{9,8},{10,9},{11,1... | collective-permute-start | bytes 196616 | tf_op jit(solution)/shard_map/ppermute | solution.py:285
  48.9 8.9 %collective-permute-start.7 = (bf16[2,27,16,128]{3,2,1,0:T(8,128)(2,1)S(1)}, bf16[2,27,16,128]{3,2,1,0:T(8,128)(2,1)S(1)}, u32[]{:S(2)}, u32[]{:S(2)}) collective-permute-start(bf16[2,27,16,128]{3,2,1,0:T(8,128)(2,1)S(1)} %fusion.3), channel_id=1, source_target_pairs={{0,4},{1,29},{2,6},{3,31},{4,8},{5,1},{6,10},{7,3},{8,12},{9,5},{1... | collective-permute-start | bytes 663560 | tf_op jit(solution)/shard_map/ppermute | solution.py:298
  49.0 20.6 %collective-permute-start.12 = (bf16[6,16,16,256]{3,2,1,0:T(8,128)(2,1)}, bf16[6,16,16,256]{3,2,1,0:T(8,128)(2,1)S(1)}, u32[]{:S(2)}, u32[]{:S(2)}) collective-permute-start(bf16[6,16,16,256]{3,2,1,0:T(8,128)(2,1)} %bitcast.38), channel_id=1, source_target_pairs={{224,0},{0,32},{32,64},{64,96},{96,128},{128,160},{160,192},{192,2... | collective-permute-start | bytes 2359304 | tf_op jit(solution)/shard_map/ppermute | solution.py:279
  58.8 7.2 %collective-permute-start.10 = (bf16[2,27,16,128]{3,2,1,0:T(8,128)(2,1)S(1)}, bf16[2,27,16,128]{3,2,1,0:T(8,128)(2,1)S(1)}, u32[]{:S(2)}, u32[]{:S(2)}) collective-permute-start(bf16[2,27,16,128]{3,2,1,0:T(8,128)(2,1)S(1)} %fusion), channel_id=1, source_target_pairs={{0,4},{1,29},{2,6},{3,31},{4,8},{5,1},{6,10},{7,3},{8,12},{9,5},{1... | collective-permute-start | bytes 663560 | tf_op jit(solution)/shard_map/ppermute | solution.py:298
  67.1 7.2 %collective-permute-start.11 = (bf16[2,27,16,128]{3,2,1,0:T(8,128)(2,1)S(1)}, bf16[2,27,16,128]{3,2,1,0:T(8,128)(2,1)S(1)}, u32[]{:S(2)}, u32[]{:S(2)}) collective-permute-start(bf16[2,27,16,128]{3,2,1,0:T(8,128)(2,1)S(1)} %fusion.1), channel_id=1, source_target_pairs={{0,4},{1,29},{2,6},{3,31},{4,8},{5,1},{6,10},{7,3},{8,12},{9,5},{1... | collective-permute-start | bytes 663560 | tf_op jit(solution)/shard_map/ppermute | solution.py:298
  75.3 8.2 %collective-permute-start.14 = (bf16[2,27,16,128]{3,2,1,0:T(8,128)(2,1)S(1)}, bf16[2,27,16,128]{3,2,1,0:T(8,128)(2,1)S(1)}, u32[]{:S(2)}, u32[]{:S(2)}) collective-permute-start(bf16[2,27,16,128]{3,2,1,0:T(8,128)(2,1)S(1)} %fusion.2), channel_id=1, source_target_pairs={{0,6},{1,3},{2,4},{3,1},{4,10},{5,7},{6,8},{7,5},{8,14},{9,11},{10... | collective-permute-start | bytes 663560 | tf_op jit(solution)/shard_map/ppermute | solution.py:298
  76.1 11.6 %collective-permute-start.13 = (bf16[2,27,16,128]{3,2,1,0:T(8,128)(2,1)S(1)}, bf16[2,27,16,128]{3,2,1,0:T(8,128)(2,1)S(1)}, u32[]{:S(2)}, u32[]{:S(2)}) collective-permute-start(bf16[2,27,16,128]{3,2,1,0:T(8,128)(2,1)S(1)} %fusion.2), channel_id=1, source_target_pairs={{0,4},{1,1},{2,6},{3,3},{4,8},{5,5},{6,10},{7,7},{8,12},{9,9},{10,... | collective-permute-start | bytes 663560 | tf_op jit(solution)/shard_map/ppermute | solution.py:298
  87.8 2.0 %collective-permute-start.15 = (bf16[2,27,16,128]{3,2,1,0:T(8,128)(2,1)S(1)}, bf16[2,27,16,128]{3,2,1,0:T(8,128)(2,1)S(1)}, u32[]{:S(2)}, u32[]{:S(2)}) collective-permute-start(bf16[2,27,16,128]{3,2,1,0:T(8,128)(2,1)S(1)} %add_convert_fusion.1), channel_id=1, source_target_pairs={{0,1},{1,0},{2,3},{3,2},{4,5},{5,4},{6,7},{7,6},{8,9},{9,8},{10,11... | collective-permute-start | bytes 663560 | tf_op jit(solution)/shard_map/ppermute | solution.py:298
  87.9 7.0 %collective-permute-start.17 = (bf16[2,16,16,256]{3,2,1,0:T(8,128)(2,1)S(1)}, bf16[2,16,16,256]{3,2,1,0:T(8,128)(2,1)S(1)}, u32[]{:S(2)}, u32[]{:S(2)}) collective-permute-start(bf16[2,16,16,256]{3,2,1,0:T(8,128)(2,1)S(1)} %get-tuple-element.90), channel_id=1, source_target_pairs={{0,1},{1,2},{2,3},{3,4},{4,5},{5,6},{6,7},{7,8},{8,9},{9,10},{10,1... | collective-permute-start | bytes 786440 | tf_op jit(solution)/shard_map/ppermute | solution.py:284
  88.5 7.8 %collective-permute-start.18 = (bf16[2,16,16,256]{3,2,1,0:T(8,128)(2,1)S(1)}, bf16[2,16,16,256]{3,2,1,0:T(8,128)(2,1)S(1)}, u32[]{:S(2)}, u32[]{:S(2)}) collective-permute-start(bf16[2,16,16,256]{3,2,1,0:T(8,128)(2,1)S(1)} %get-tuple-element.89), channel_id=1, source_target_pairs={{1,0},{2,1},{3,2},{4,3},{5,4},{6,5},{7,6},{8,7},{9,8},{10,9},{11,1... | collective-permute-start | bytes 786440 | tf_op jit(solution)/shard_map/ppermute | solution.py:285
  89.8 7.2 %collective-permute-start.16 = (bf16[2,27,16,128]{3,2,1,0:T(8,128)(2,1)S(1)}, bf16[2,27,16,128]{3,2,1,0:T(8,128)(2,1)S(1)}, u32[]{:S(2)}, u32[]{:S(2)}) collective-permute-start(bf16[2,27,16,128]{3,2,1,0:T(8,128)(2,1)S(1)} %add_convert_fusion.refs_0_), channel_id=1, source_target_pairs={{0,4},{1,29},{2,6},{3,31},{4,8},{5,1},{6,10},{7,3},{8,12},{9,5},{1... | collective-permute-start | bytes 663560 | tf_op jit(solution)/shard_map/ppermute | solution.py:298
  97.0 8.1 %collective-permute-start.19 = (bf16[2,27,16,128]{3,2,1,0:T(8,128)(2,1)S(1)}, bf16[2,27,16,128]{3,2,1,0:T(8,128)(2,1)S(1)}, u32[]{:S(2)}, u32[]{:S(2)}) collective-permute-start(bf16[2,27,16,128]{3,2,1,0:T(8,128)(2,1)S(1)} %collective-permute-done.16.refs_1_), channel_id=1, source_target_pairs={{0,4},{1,29},{2,6},{3,31},{4,8},{5,1},{6,10},{7,3},{8,12},{9,5},{1... | collective-permute-start | bytes 663560 | tf_op jit(solution)/shard_map/ppermute | solution.py:298
  97.0 8.1 %collective-permute-start.20 = (bf16[2,27,16,128]{3,2,1,0:T(8,128)(2,1)S(1)}, bf16[2,27,16,128]{3,2,1,0:T(8,128)(2,1)S(1)}, u32[]{:S(2)}, u32[]{:S(2)}) collective-permute-start(bf16[2,27,16,128]{3,2,1,0:T(8,128)(2,1)S(1)} %collective-permute-done.16.refs_1_), channel_id=1, source_target_pairs={{0,1},{1,0},{2,3},{3,2},{4,5},{5,4},{6,7},{7,6},{8,9},{9,8},{10,11... | collective-permute-start | bytes 663560 | tf_op jit(solution)/shard_map/ppermute | solution.py:298
  105.2 8.4 %copy-start = (f32[1,2,27,128,128]{4,3,2,1,0:T(8,128)S(1)}, f32[1,2,27,128,128]{4,3,2,1,0:T(8,128)}, u32[]{:S(2)}) copy-start(f32[1,2,27,128,128]{4,3,2,1,0:T(8,128)} %momentum.3) | copy-start | bytes 10616836
  105.2 7.2 %collective-permute-start.21 = (bf16[2,27,16,128]{3,2,1,0:T(8,128)(2,1)S(1)}, bf16[2,27,16,128]{3,2,1,0:T(8,128)(2,1)S(1)}, u32[]{:S(2)}, u32[]{:S(2)}) collective-permute-start(bf16[2,27,16,128]{3,2,1,0:T(8,128)(2,1)S(1)} %collective-permute-done.19.refs_3_), channel_id=1, source_target_pairs={{0,4},{1,29},{2,6},{3,31},{4,8},{5,1},{6,10},{7,3},{8,12},{9,5},{1... | collective-permute-start | bytes 663560 | tf_op jit(solution)/shard_map/ppermute | solution.py:298
  105.3 7.1 %collective-permute-start.22 = (bf16[2,27,16,128]{3,2,1,0:T(8,128)(2,1)S(1)}, bf16[2,27,16,128]{3,2,1,0:T(8,128)(2,1)S(1)}, u32[]{:S(2)}, u32[]{:S(2)}) collective-permute-start(bf16[2,27,16,128]{3,2,1,0:T(8,128)(2,1)S(1)} %collective-permute-done.19.refs_3_), channel_id=1, source_target_pairs={{0,1},{1,0},{2,3},{3,2},{4,5},{5,4},{6,7},{7,6},{8,9},{9,8},{10,11... | collective-permute-start | bytes 663560 | tf_op jit(solution)/shard_map/ppermute | solution.py:298
  112.4 7.1 %collective-permute-start.23 = (bf16[2,27,16,128]{3,2,1,0:T(8,128)(2,1)S(1)}, bf16[2,27,16,128]{3,2,1,0:T(8,128)(2,1)S(1)}, u32[]{:S(2)}, u32[]{:S(2)}) collective-permute-start(bf16[2,27,16,128]{3,2,1,0:T(8,128)(2,1)S(1)} %collective-permute-done.21.refs_0_), channel_id=1, source_target_pairs={{0,4},{1,29},{2,6},{3,31},{4,8},{5,1},{6,10},{7,3},{8,12},{9,5},{1... | collective-permute-start | bytes 663560 | tf_op jit(solution)/shard_map/ppermute | solution.py:298
  112.4 7.1 %collective-permute-start.24 = (bf16[2,27,16,128]{3,2,1,0:T(8,128)(2,1)S(1)}, bf16[2,27,16,128]{3,2,1,0:T(8,128)(2,1)S(1)}, u32[]{:S(2)}, u32[]{:S(2)}) collective-permute-start(bf16[2,27,16,128]{3,2,1,0:T(8,128)(2,1)S(1)} %collective-permute-done.21.refs_0_), channel_id=1, source_target_pairs={{0,1},{1,0},{2,3},{3,2},{4,5},{5,4},{6,7},{7,6},{8,9},{9,8},{10,11... | collective-permute-start | bytes 663560 | tf_op jit(solution)/shard_map/ppermute | solution.py:298
where the time goes:
time: 122 us
  Pallas kernels  48.4 us (40%)
  waiting for transfers between devices  33.5 us (27%)
  starting transfers between devices  30.3 us (25%)
  local copies, waits for them, and re-layouts  4.4 us (4%)
  other arithmetic  4.3 us (4%)
    ppermute x14, waiting for transfers between devices, sent(): return lax.ppermute(block, 'tile', tiles(target))  28.3 us
    ppermute x4, starting transfers between devices, halo(): lax.ppermute(high_block, 'tile', [((i + 1) % count, i) for i in range(cou...  10.6 us
    ppermute x14, starting transfers between devices, sent(): return lax.ppermute(block, 'tile', tiles(target))  9.76 us
    ppermute x3, starting transfers between devices, along(): lax.ppermute(block, 'section', [((i - distance) % count, i) for i in rang...  8.49 us
    pallas_call x1, Pallas kernels, shards(): call(first_kernel, [SMEM] + [VMEM] * 7 + [anywhere] * 2, [whole, (field,...  7.17 us
    pallas_call x1, Pallas kernels, shards(): call(stored_kernel, [SMEM, VMEM, VMEM, VMEM, taps_of(1)], [((8, CELLS, ha...  6.36 us
    pallas_call x1, Pallas kernels, shards(): call(inner_kernel, [SMEM, VMEM, VMEM, VMEM, VMEM, taps_of(0)], [((6, CELL...  5.98 us
    pallas_call x2, Pallas kernels, updated(): pl.pallas_call(functools.partial(momentum_kernel, scale, count), grid_spe...  5.53 us
  transfers between devices with their start and end apart: 25, of which 13 were waited for; matrix products, arithmetic and copies ran while one was open for 5% of the time, Pallas kernels for 32%

commit v1 on v0

--- a/solution.py
+++ b/solution.py
@@ -112,6 +112,15 @@
             r_out[at + h] = jnp.where(outside(place, at + h), 0.0, two).astype(bf16)
 
     pairs(8, step)
+
+
+def cut_kernel(z, c, top, bottom, c_one, c_two):
+    for at in range(2):
+        top[at] = z[at + 4]
+        bottom[at] = z[at]
+    for at in range(6):
+        c_one[at] = c[at, :, :, 0:128]
+        c_two[at] = c[at, :, :, 128:256]
 
 
 def turned_kernel(w, w_turned):
@@ -347,9 +356,14 @@
     anywhere = pl.BlockSpec(memory_space=pl.ANY)
 
     z = stored_out[0]
-    c_two = along(cotangent[0, ..., half:], -1)
-    z_low, z_high = halo(z[4:], z[:2])
+    ends = ((2, 16, 16, 2 * half), bf16)
+    top, bottom, c_one, c_two = call(cut_kernel, [VMEM, VMEM], [ends, ends, (field, bf16), (field, bf16)], [], 1)(
+        z, cotangent[0]
+    )
+    z_low, z_high = halo(top, bottom)
     (g_turned,) = call(turned_kernel, [taps_of(1)], [taps], [], 1)(weights)
+    c_two, g_turned = tied(c_two, g_turned)
+    c_two = along(c_two, -1)
     z_low, z_high, g_turned = tied(z_low, z_high, g_turned)
     g_scale, r = call(
         stored_kernel,
@@ -358,7 +372,7 @@
         [wide10, taps, ten, eight],
         8,
     )(place, z, z_low, z_high, weights)
-    late, r = tied(cotangent[0, ..., :half], r)
+    late, r = tied(c_one, r)
     c_one = along(late, -1)
     pg = (c_two.astype(f32) * g_scale[1:7].reshape(field)).astype(bf16)
     pg, r = tied(pg, r)
@@ -403,13 +417,15 @@
     steps = jnp.stack([0 * sign, sign, -sign, 2 * sign, -2 * sign, 3 * sign, -3 * sign, 4 * sign])
     places = (deep + steps + 32) % 8
     got = onward(own(0).astype(bf16))
+    owned = [own(m) for m in (1, 2, 3)]
     (f_turned,) = call(turned_kernel, [taps_of(0)], [taps], [], 1)(weights_later)
-    got, places, f_turned, pf_low, pf_high = tied(got, places, f_turned, pf_low, pf_high)
-    got = onward((own(1) + got.astype(f32)).astype(bf16))
-    got = onward((own(2) + got.astype(f32)).astype(bf16))
+    got, places, pf_low, pf_high, *owned = tied(got, places, pf_low, pf_high, *owned)
+    got = onward((owned[0] + got.astype(f32)).astype(bf16))
+    got, f_turned = tied(got, f_turned)
+    got = onward((owned[1] + got.astype(f32)).astype(bf16))
     got, a = tied(got, a)
     a_low, a_high = halo(a[4:], a[:2])
-    held = (own(3) + got.astype(f32)).astype(bf16)
+    held = (owned[2] + got.astype(f32)).astype(bf16)
     straight = sent(held, lambda z, y, c: (z + 1 - c, y, c))
     across = sent(held, lambda z, y, c: (z + 1 - c, 1 - y, c))
     held = (straight.astype(f32) + across.astype(f32)).astype(bf16)

time: 122 us -> 120 us (0.984)
  waiting for transfers between devices: 33.5 us -> 36.1 us
  other arithmetic: 4.3 us -> 1.88 us
  starting transfers between devices: 30.3 us -> 28.3 us
    unnamed x8 -> x16, local copies, waits for them, and re-layouts: 0.02 us -> 5.22 us
    convert_element_type x4 -> x3, other arithmetic: 4.08 us -> 0.19 us  [the longest x1 0.07 us: shards(): got = onward((owned[0] + got.astype(f32)).astype(bf16))]
    ppermute x3, waiting for transfers between devices: 3.42 us -> 7.01 us  [along(): lax.ppermute(block, 'section', [((i - distance) % count, i) for i in rang...]
    ppermute x14, waiting for transfers between devices: 28.3 us -> 26 us  [sent(): return lax.ppermute(block, 'tile', tiles(target))]
    squeeze x1 -> x0, local copies, waits for them, and re-layouts: 2.13 us -> none  [shards(): late, r = tied(cotangent[0, ..., :half], r)]
    slice x1 -> x0, local copies, waits for them, and re-layouts: 1.99 us -> none  [shards(): z_low, z_high = halo(z[4:], z[:2])]
    ppermute x4, starting transfers between devices: 10.6 us -> 8.92 us  [halo(): lax.ppermute(high_block, 'tile', [((i + 1) % count, i) for i in range(cou...]
    add x0 -> x1, other arithmetic: none -> 1.45 us  [own(): return mine[m].astype(f32) + from_core[m].astype(f32)]
  transfers between devices with their start and end apart: 25 -> 25, of which waited for: 13 -> 13; matrix products, arithmetic and copies ran while one was open for 5% -> 2% of each run, Pallas kernels for 32% -> 31%
where the time goes in v1:
time: 120 us
  Pallas kernels  47.5 us (40%)
  waiting for transfers between devices  36.1 us (30%)
  starting transfers between devices  28.3 us (24%)
  local copies, waits for them, and re-layouts  5.49 us (5%)
  other arithmetic  1.88 us (2%)
    ppermute x14, waiting for transfers between devices, sent(): return lax.ppermute(block, 'tile', tiles(target))  26 us
    ppermute x14, starting transfers between devices, sent(): return lax.ppermute(block, 'tile', tiles(target))  9.35 us
    ppermute x4, starting transfers between devices, halo(): lax.ppermute(high_block, 'tile', [((i + 1) % count, i) for i in range(cou...  8.92 us
    ppermute x3, starting transfers between devices, along(): lax.ppermute(block, 'section', [((i - distance) % count, i) for i in rang...  8.26 us
    pallas_call x1, Pallas kernels, shards(): call(first_kernel, [SMEM] + [VMEM] * 7 + [anywhere] * 2, [whole, (field,...  7.19 us
    ppermute x3, waiting for transfers between devices, along(): lax.ppermute(block, 'section', [((i - distance) % count, i) for i in rang...  7.01 us
    pallas_call x2, Pallas kernels, updated(): pl.pallas_call(functools.partial(momentum_kernel, scale, count), grid_spe...  5.53 us
    pallas_call x1, Pallas kernels, shards(): call(stored_kernel, [SMEM, VMEM, VMEM, VMEM, taps_of(1)], [((8, CELLS, ha...  5.35 us
  transfers between devices with their start and end apart: 25, of which 13 were waited for; matrix products, arithmetic and copies ran while one was open for 2% of the time, Pallas kernels for 31%

profile of v1, /device:TPU:8, one launch (start us, length us, event | category | flops | bytes accessed | tf_op | source)
XLA Modules:
  0.0 120.1 jit_solution(6286755426152753331)
XLA Ops:
  3.9 1.7 %collective-permute-start.2 = (bf16[2,16,16,256]{3,2,1,0:T(8,128)(2,1)}, bf16[2,16,16,256]{3,2,1,0:T(8,128)(2,1)S(1)}, u32[]{:S(2)}, u32[]{:S(2)}) collective-permute-start(bf16[2,16,16,256]{3,2,1,0:T(8,128)(2,1)} %get-tuple-element.59), channel_id=1, source_target_pairs={{1,0},{2,1},{3,2},{4,3},{5,4},{6,5},{7,6},{8,7},{9,8},{10,9},{11,1... | collective-permute-start | bytes 786440 | tf_op jit(solution)/shard_map/ppermute | solution.py:294
  5.6 1.5 %copy-done.1 = bf16[1,2,27,128,128]{4,3,2,1,0:T(8,128)(2,1)S(1)} copy-done((bf16[1,2,27,128,128]{4,3,2,1,0:T(8,128)(2,1)S(1)}, bf16[1,2,27,128,128]{4,3,2,1,0:T(8,128)(2,1)}, u32[]{:S(2)}) %copy-start.1) | copy-done | bytes 1769496
  7.1 2.7 %shard_map.77.taps = bf16[3456,128]{1,0:T(8,128)(2,1)S(1)} custom-call(bf16[1,2,27,128,128]{4,3,2,1,0:T(8,128)(2,1)S(1)} %copy-done.1), custom_call_target="tpu_custom_call" | custom-call | flops 226492416 | bytes 6000000 | tf_op jit(solution)/shard_map/pallas_call | solution.py:364
  9.8 4.6 %collective-permute-start = (bf16[6,16,16,128]{3,2,1,0:T(8,128)(2,1)S(1)}, bf16[6,16,16,128]{3,2,1,0:T(8,128)(2,1)S(1)}, u32[]{:S(2)}, u32[]{:S(2)}) collective-permute-start(bf16[6,16,16,128]{3,2,1,0:T(8,128)(2,1)S(1)} %get-tuple-element.57), channel_id=1, source_target_pairs={{32,0},{64,32},{96,64},{128,96},{160,128},{192,160},{224,192},{0,2... | collective-permute-start | bytes 1179656 | tf_op jit(solution)/shard_map/ppermute | solution.py:288
  14.4 1.5 %copy-done.2 = bf16[1,2,27,128,128]{4,3,2,1,0:T(8,128)(2,1)S(1)} copy-done((bf16[1,2,27,128,128]{4,3,2,1,0:T(8,128)(2,1)S(1)}, bf16[1,2,27,128,128]{4,3,2,1,0:T(8,128)(2,1)}, u32[]{:S(2)}) %copy-start.2) | copy-done | bytes 1769496
  15.9 5.4 %shard_map.78 = (f32[8,256,128]{2,1,0:T(8,128)S(1)}, bf16[8,256,128]{2,1,0:T(8,128)(2,1)S(1)}) custom-call(s32[1]{0:T(128)} %bitcast.place, bf16[6,16,16,256]{3,2,1,0:T(8,128)(2,1)S(1)} %bitcast.23, bf16[2,16,16,256]{3,2,1,0:T(8,128)(2,1)S(1)} %collective-permute-done.1.z_low, bf16[2,16,16,256]{3,2,1,0:T(8,128)(2,1)S(1)} %collective-permute-done.2.z_high, ...), custom_call_target="tpu_custom_call" | custom-call | flops 1811939328 | bytes 6000000 | tf_op jit(solution)/shard_map/pallas_call | solution.py:368
  21.3 1.3 %collective-permute-start.5 = (bf16[6,16,16,128]{3,2,1,0:T(8,128)(2,1)S(1)}, bf16[6,16,16,128]{3,2,1,0:T(8,128)(2,1)S(1)}, u32[]{:S(2)}, u32[]{:S(2)}) collective-permute-start(bf16[6,16,16,128]{3,2,1,0:T(8,128)(2,1)S(1)} %get-tuple-element.70), channel_id=1, source_target_pairs={{32,0},{64,32},{96,64},{128,96},{160,128},{192,160},{224,192},{0,2... | collective-permute-start | bytes 1179656 | tf_op jit(solution)/shard_map/ppermute | solution.py:288
  24.5 2.3 %collective-permute-start.4 = (bf16[1,16,16,128]{3,2,1,0:T(8,128)(2,1)S(1)}, bf16[1,16,16,128]{3,2,1,0:T(8,128)(2,1)S(1)}, u32[]{:S(2)}, u32[]{:S(2)}) collective-permute-start(bf16[1,16,16,128]{3,2,1,0:T(8,128)(2,1)S(1)} %get-tuple-element.117), channel_id=1, source_target_pairs={{1,0},{2,1},{3,2},{4,3},{5,4},{6,5},{7,6},{8,7},{9,8},{10,9},{11,1... | collective-permute-start | bytes 196616 | tf_op jit(solution)/shard_map/ppermute | solution.py:294
  26.7 5.0 %shard_map.79 = (f32[6,256,128]{2,1,0:T(8,128)S(1)}, bf16[384,2048]{1,0:T(8,128)(2,1)S(1)}, bf16[384,2048]{1,0:T(8,128)(2,1)S(1)}) custom-call(s32[1]{0:T(128)} %bitcast.place, bf16[6,16,16,256]{3,2,1,0:T(8,128)(2,1)S(1)} %bitcast.24, bf16[2,16,16,256]{3,2,1,0:T(8,128)(2,1)S(1)} %collective-permute-done.1.z_low, ...), custom_call_target="tpu_custom_call" | custom-call | flops 1358954496 | bytes 6000000 | tf_op jit(solution)/shard_map/pallas_call | solution.py:380
  31.8 3.2 %shard_map.80 = (bf16[4,2,27,16,128]{4,3,2,1,0:T(8,128)(2,1)S(1)}, bf16[4,2,27,16,128]{4,3,2,1,0:T(8,128)(2,1)}) custom-call(s32[1]{0:T(128)} %bitcast.place, bf16[384,2048]{1,0:T(8,128)(2,1)S(1)} %get-tuple-element.75.z_flat, bf16[6,16,16,128]{3,2,1,0:T(8,128)(2,1)S(1)} %multiply_convert_fusion.pg), custom_call_target="tpu_custom_call" | custom-call | flops 1358954496 | bytes 6000000 | tf_op jit(solution)/shard_map/pallas_call | solution.py:394
  36.2 7.2 %shard_map.81 = (bf16[1,6,16,16,256]{4,3,2,1,0:T(8,128)(2,1)}, bf16[6,16,16,128]{3,2,1,0:T(8,128)(2,1)S(1)}, bf16[4,2,27,16,128]{4,3,2,1,0:T(8,128)(2,1)S(1)}, bf16[4,2,27,16,128]{4,3,2,1,0:T(8,128)(2,1)}) custom-call(s32[1]{0:T(128)} %bitcast.place, ...), custom_call_target="tpu_custom_call", output_to_operand_aliasing={{2}: (8, {}), {3}: (9, {})} | custom-call | flops 2717908992 | bytes 6000000 | tf_op jit(solution)/shard_map/pallas_call | solution.py:399
  44.1 3.7 %collective-permute-start.9 = (bf16[1,16,16,128]{3,2,1,0:T(8,128)(2,1)S(1)}, bf16[1,16,16,128]{3,2,1,0:T(8,128)(2,1)S(1)}, u32[]{:S(2)}, u32[]{:S(2)}) collective-permute-start(bf16[1,16,16,128]{3,2,1,0:T(8,128)(2,1)S(1)} %get-tuple-element.115), channel_id=1, source_target_pairs={{1,0},{2,1},{3,2},{4,3},{5,4},{6,5},{7,6},{8,7},{9,8},{10,9},{11,1... | collective-permute-start | bytes 196616 | tf_op jit(solution)/shard_map/ppermute | solution.py:294
  47.8 1.5 %add_bitcast_fusion = (f32[2,27,16,128]{3,2,1,0:T(8,128)S(1)}, f32[2,27,16,128]{3,2,1,0:T(8,128)S(1)}, f32[2,27,16,128]{3,2,1,0:T(8,128)S(1)}, bf16[2,27,16,128]{3,2,1,0:T(8,128)(2,1)S(1)}) fusion(bf16[4,2,27,16,128]{4,3,2,1,0:T(8,128)(2,1)} %collective-permute-done.6, bf16[4,2,27,16,128]{4,3,2,1,0:T(8,128)(2,1)S(1)} %get-tuple-element.78), kind=kLoop, calls=%fused_computation.6 | loop fusion | flops 1437696 | bytes 3317760 | tf_op jit(solution)/shard_map/add | solution.py:414
  49.3 2.4 %collective-permute-start.12 = (bf16[6,16,16,256]{3,2,1,0:T(8,128)(2,1)S(1)}, bf16[6,16,16,256]{3,2,1,0:T(8,128)(2,1)S(1)}, u32[]{:S(2)}, u32[]{:S(2)}) collective-permute-start(bf16[6,16,16,256]{3,2,1,0:T(8,128)(2,1)S(1)} %bitcast.27), channel_id=1, source_target_pairs={{224,0},{0,32},{32,64},{64,96},{96,128},{128,160},{160,192},{192,2... | collective-permute-start | bytes 2359304 | tf_op jit(solution)/shard_map/ppermute | solution.py:288
  51.7 5.5 %collective-permute-done.7 = bf16[2,27,16,128]{3,2,1,0:T(8,128)(2,1)S(1)} collective-permute-done((bf16[2,27,16,128]{3,2,1,0:T(8,128)(2,1)S(1)}, bf16[2,27,16,128]{3,2,1,0:T(8,128)(2,1)S(1)}, u32[]{:S(2)}, u32[]{:S(2)}) %collective-permute-start.7) | collective-permute-done | bytes 221216 | tf_op jit(solution)/shard_map/ppermute | solution.py:307
  57.4 2.7 %shard_map.82.taps = bf16[3456,128]{1,0:T(8,128)(2,1)S(1)} custom-call(bf16[1,2,27,128,128]{4,3,2,1,0:T(8,128)(2,1)S(1)} %copy-done.3), custom_call_target="tpu_custom_call" | custom-call | flops 226492416 | bytes 6000000 | tf_op jit(solution)/shard_map/pallas_call | solution.py:421
  60.1 4.4 %collective-permute-done.10 = bf16[2,27,16,128]{3,2,1,0:T(8,128)(2,1)S(1)} collective-permute-done((bf16[2,27,16,128]{3,2,1,0:T(8,128)(2,1)S(1)}, bf16[2,27,16,128]{3,2,1,0:T(8,128)(2,1)S(1)}, u32[]{:S(2)}, u32[]{:S(2)}) %collective-permute-start.10) | collective-permute-done | bytes 221216 | tf_op jit(solution)/shard_map/ppermute | solution.py:307
  64.7 5.9 %collective-permute-done.12.a = bf16[6,16,16,256]{3,2,1,0:T(8,128)(2,1)S(1)} collective-permute-done((bf16[6,16,16,256]{3,2,1,0:T(8,128)(2,1)S(1)}, bf16[6,16,16,256]{3,2,1,0:T(8,128)(2,1)S(1)}, u32[]{:S(2)}, u32[]{:S(2)}) %collective-permute-start.12) | collective-permute-done | bytes 786464 | tf_op jit(solution)/shard_map/ppermute | solution.py:288
  71.9 2.3 %collective-permute-start.14 = (bf16[2,27,16,128]{3,2,1,0:T(8,128)(2,1)S(1)}, bf16[2,27,16,128]{3,2,1,0:T(8,128)(2,1)S(1)}, u32[]{:S(2)}, u32[]{:S(2)}) collective-permute-start(bf16[2,27,16,128]{3,2,1,0:T(8,128)(2,1)S(1)} %add_convert_fusion.2), channel_id=1, source_target_pairs={{0,6},{1,3},{2,4},{3,1},{4,10},{5,7},{6,8},{7,5},{8,14},{9,11},{10... | collective-permute-start | bytes 663560 | tf_op jit(solution)/shard_map/ppermute | solution.py:307
  74.2 2.0 %collective-permute-start.13 = (bf16[2,27,16,128]{3,2,1,0:T(8,128)(2,1)S(1)}, bf16[2,27,16,128]{3,2,1,0:T(8,128)(2,1)S(1)}, u32[]{:S(2)}, u32[]{:S(2)}) collective-permute-start(bf16[2,27,16,128]{3,2,1,0:T(8,128)(2,1)S(1)} %add_convert_fusion.2), channel_id=1, source_target_pairs={{0,4},{1,1},{2,6},{3,3},{4,8},{5,5},{6,10},{7,7},{8,12},{9,9},{10,... | collective-permute-start | bytes 663560 | tf_op jit(solution)/shard_map/ppermute | solution.py:307
  76.2 4.9 %collective-permute-done.14 = bf16[2,27,16,128]{3,2,1,0:T(8,128)(2,1)S(1)} collective-permute-done((bf16[2,27,16,128]{3,2,1,0:T(8,128)(2,1)S(1)}, bf16[2,27,16,128]{3,2,1,0:T(8,128)(2,1)S(1)}, u32[]{:S(2)}, u32[]{:S(2)}) %collective-permute-start.14) | collective-permute-done | bytes 221216 | tf_op jit(solution)/shard_map/ppermute | solution.py:307
  81.1 4.8 %collective-permute-done.13 = bf16[2,27,16,128]{3,2,1,0:T(8,128)(2,1)S(1)} collective-permute-done((bf16[2,27,16,128]{3,2,1,0:T(8,128)(2,1)S(1)}, bf16[2,27,16,128]{3,2,1,0:T(8,128)(2,1)S(1)}, u32[]{:S(2)}, u32[]{:S(2)}) %collective-permute-start.13) | collective-permute-done | bytes 221216 | tf_op jit(solution)/shard_map/ppermute | solution.py:307
  86.8 1.3 %collective-permute-start.18 = (bf16[2,16,16,256]{3,2,1,0:T(8,128)(2,1)S(1)}, bf16[2,16,16,256]{3,2,1,0:T(8,128)(2,1)S(1)}, u32[]{:S(2)}, u32[]{:S(2)}) collective-permute-start(bf16[2,16,16,256]{3,2,1,0:T(8,128)(2,1)S(1)} %get-tuple-element.113), channel_id=1, source_target_pairs={{1,0},{2,1},{3,2},{4,3},{5,4},{6,5},{7,6},{8,7},{9,8},{10,9},{11,1... | collective-permute-start | bytes 786440 | tf_op jit(solution)/shard_map/ppermute | solution.py:294
  88.2 4.6 %shard_map.83 = bf16[1,6,16,16,256]{4,3,2,1,0:T(8,128)(2,1)} custom-call(s32[1]{0:T(128)} %bitcast.place, bf16[6,16,16,128]{3,2,1,0:T(8,128)(2,1)S(1)} %get-tuple-element.81.pf, bf16[1,16,16,128]{3,2,1,0:T(8,128)(2,1)S(1)} %collective-permute-done.8.pf_low, ...), custom_call_target="tpu_custom_call", output_to_operand_aliasing={{}: (6, {})} | custom-call | flops 1358954496 | bytes 6000000 | tf_op jit(solution)/shard_map/pallas_call | solution.py:434
  93.2 1.4 %collective-permute-done.18.a_high = bf16[2,16,16,256]{3,2,1,0:T(8,128)(2,1)S(1)} collective-permute-done((bf16[2,16,16,256]{3,2,1,0:T(8,128)(2,1)S(1)}, bf16[2,16,16,256]{3,2,1,0:T(8,128)(2,1)S(1)}, u32[]{:S(2)}, u32[]{:S(2)}) %collective-permute-start.18) | collective-permute-done | bytes 262176 | tf_op jit(solution)/shard_map/ppermute | solution.py:294
  95.3 2.8 %collective-permute-start.20 = (bf16[2,27,16,128]{3,2,1,0:T(8,128)(2,1)S(1)}, bf16[2,27,16,128]{3,2,1,0:T(8,128)(2,1)S(1)}, u32[]{:S(2)}, u32[]{:S(2)}) collective-permute-start(bf16[2,27,16,128]{3,2,1,0:T(8,128)(2,1)S(1)} %collective-permute-done.16.refs_1_), channel_id=1, source_target_pairs={{0,1},{1,0},{2,3},{3,2},{4,5},{5,4},{6,7},{7,6},{8,9},{9,8},{10,11... | collective-permute-start | bytes 663560 | tf_op jit(solution)/shard_map/ppermute | solution.py:307
  98.1 5.4 %shard_map.84.b = bf16[8,256,128]{2,1,0:T(8,128)(2,1)S(1)} custom-call(s32[1]{0:T(128)} %bitcast.place, bf16[6,16,16,256]{3,2,1,0:T(8,128)(2,1)S(1)} %collective-permute-done.12.a, bf16[2,16,16,256]{3,2,1,0:T(8,128)(2,1)S(1)} %collective-permute-done.17.a_low, bf16[2,16,16,256]{3,2,1,0:T(8,128)(2,1)S(1)} %collective-permute-done.18.a_high, ...), custom_call_target="tpu_custom_call" | custom-call | flops 1811939328 | bytes 6000000 | tf_op jit(solution)/shard_map/pallas_call | solution.py:440
  104.2 4.7 %shard_map.85 = bf16[1,6,16,16,256]{4,3,2,1,0:T(8,128)(2,1)} custom-call(bf16[6,16,16,256]{3,2,1,0:T(8,128)(2,1)S(1)} %collective-permute-done.12.a, bf16[8,256,128]{2,1,0:T(8,128)(2,1)S(1)} %shard_map.84.b, bf16[1,2,27,128,128]{4,3,2,1,0:T(8,128)(2,1)S(1)} %copy-done.3), custom_call_target="tpu_custom_call" | custom-call | flops 1358954496 | bytes 6000000 | tf_op jit(solution)/shard_map/pallas_call | solution.py:446
  109.0 1.7 %collective-permute-done.21.refs_0_ = bf16[2,27,16,128]{3,2,1,0:T(8,128)(2,1)S(1)} collective-permute-done((bf16[2,27,16,128]{3,2,1,0:T(8,128)(2,1)S(1)}, bf16[2,27,16,128]{3,2,1,0:T(8,128)(2,1)S(1)}, u32[]{:S(2)}, u32[]{:S(2)}) %collective-permute-start.21) | collective-permute-done | bytes 221216 | tf_op jit(solution)/shard_map/ppermute | solution.py:307
  111.8 3.2 %shard_map.86.refs_3_ = f32[1,2,27,128,128]{4,3,2,1,0:T(8,128)} custom-call(s32[5]{0:T(128)S(1)} %bitcast.25, f32[1,2,27,128,128]{4,3,2,1,0:T(8,128)S(1)} %copy-done, bf16[2,27,16,128]{3,2,1,0:T(8,128)(2,1)S(1)} %add_convert_fusion.refs_0_, bf16[2,27,16,128]{3,2,1,0:T(8,128)(2,1)S(1)} %collective-permute-done.16.refs_1_, ...), custom_call_target="tpu_custom_call" | custom-call | flops 1000000 | bytes 5500000 | tf_op jit(solution)/shard_map/pallas_call | solution.py:326
  115.0 2.8 %collective-permute-done.23.refs_2_ = bf16[2,27,16,128]{3,2,1,0:T(8,128)(2,1)S(1)} collective-permute-done((bf16[2,27,16,128]{3,2,1,0:T(8,128)(2,1)S(1)}, bf16[2,27,16,128]{3,2,1,0:T(8,128)(2,1)S(1)}, u32[]{:S(2)}, u32[]{:S(2)}) %collective-permute-start.23) | collective-permute-done | bytes 221216 | tf_op jit(solution)/shard_map/ppermute | solution.py:307
  117.8 2.3 %shard_map.87 = f32[1,2,27,128,128]{4,3,2,1,0:T(8,128)} custom-call(s32[3]{0:T(128)S(1)} %slice.66.places, f32[1,2,27,128,128]{4,3,2,1,0:T(8,128)S(1)} %copy-done, bf16[2,27,16,128]{3,2,1,0:T(8,128)(2,1)S(1)} %collective-permute-done.21.refs_0_, bf16[2,27,16,128]{3,2,1,0:T(8,128)(2,1)S(1)} %collective-permute-done.24.refs_1_, ...), custom_call_target="tpu_custom_call", output_to_operand_aliasing={{}: (5, {})} | custom-call | flops 1000000 | bytes 3300000 | tf_op jit(solution)/shard_map/pallas_call | solution.py:326
  (60 shorter events, 12.6 us)
Async XLA Ops:
  0.6 1.1 copy-start.4
  2.9 11.5 %copy-start.6 = (bf16[1,6,16,16,256]{4,3,2,1,0:T(8,128)(2,1)S(1)}, bf16[1,6,16,16,256]{4,3,2,1,0:T(8,128)(2,1)}, u32[]{:S(2)}) copy-start(bf16[1,6,16,16,256]{4,3,2,1,0:T(8,128)(2,1)} %param.6) | copy-start | bytes 2359300
  3.9 10.5 %collective-permute-start.1 = (bf16[2,16,16,256]{3,2,1,0:T(8,128)(2,1)}, bf16[2,16,16,256]{3,2,1,0:T(8,128)(2,1)S(1)}, u32[]{:S(2)}, u32[]{:S(2)}) collective-permute-start(bf16[2,16,16,256]{3,2,1,0:T(8,128)(2,1)} %get-tuple-element.58), channel_id=1, source_target_pairs={{0,1},{1,2},{2,3},{3,4},{4,5},{5,6},{6,7},{7,8},{8,9},{9,10},{10,1... | collective-permute-start | bytes 786440 | tf_op jit(solution)/shard_map/ppermute | solution.py:293
  3.9 10.5 %collective-permute-start.2 = (bf16[2,16,16,256]{3,2,1,0:T(8,128)(2,1)}, bf16[2,16,16,256]{3,2,1,0:T(8,128)(2,1)S(1)}, u32[]{:S(2)}, u32[]{:S(2)}) collective-permute-start(bf16[2,16,16,256]{3,2,1,0:T(8,128)(2,1)} %get-tuple-element.59), channel_id=1, source_target_pairs={{1,0},{2,1},{3,2},{4,3},{5,4},{6,5},{7,6},{8,7},{9,8},{10,9},{11,1... | collective-permute-start | bytes 786440 | tf_op jit(solution)/shard_map/ppermute | solution.py:294
  5.6 1.5 %copy-start.1 = (bf16[1,2,27,128,128]{4,3,2,1,0:T(8,128)(2,1)S(1)}, bf16[1,2,27,128,128]{4,3,2,1,0:T(8,128)(2,1)}, u32[]{:S(2)}) copy-start(bf16[1,2,27,128,128]{4,3,2,1,0:T(8,128)(2,1)} %w_g.3) | copy-start | bytes 5308420
  9.8 13.9 %collective-permute-start = (bf16[6,16,16,128]{3,2,1,0:T(8,128)(2,1)S(1)}, bf16[6,16,16,128]{3,2,1,0:T(8,128)(2,1)S(1)}, u32[]{:S(2)}, u32[]{:S(2)}) collective-permute-start(bf16[6,16,16,128]{3,2,1,0:T(8,128)(2,1)S(1)} %get-tuple-element.57), channel_id=1, source_target_pairs={{32,0},{64,32},{96,64},{128,96},{160,128},{192,160},{224,192},{0,2... | collective-permute-start | bytes 1179656 | tf_op jit(solution)/shard_map/ppermute | solution.py:288
  14.4 1.5 %copy-start.2 = (bf16[1,2,27,128,128]{4,3,2,1,0:T(8,128)(2,1)S(1)}, bf16[1,2,27,128,128]{4,3,2,1,0:T(8,128)(2,1)}, u32[]{:S(2)}) copy-start(bf16[1,2,27,128,128]{4,3,2,1,0:T(8,128)(2,1)} %w_g.3) | copy-start | bytes 5308420
  21.3 14.9 %collective-permute-start.5 = (bf16[6,16,16,128]{3,2,1,0:T(8,128)(2,1)S(1)}, bf16[6,16,16,128]{3,2,1,0:T(8,128)(2,1)S(1)}, u32[]{:S(2)}, u32[]{:S(2)}) collective-permute-start(bf16[6,16,16,128]{3,2,1,0:T(8,128)(2,1)S(1)} %get-tuple-element.70), channel_id=1, source_target_pairs={{32,0},{64,32},{96,64},{128,96},{160,128},{192,160},{224,192},{0,2... | collective-permute-start | bytes 1179656 | tf_op jit(solution)/shard_map/ppermute | solution.py:288
  23.8 12.4 %collective-permute-start.3 = (bf16[1,16,16,128]{3,2,1,0:T(8,128)(2,1)S(1)}, bf16[1,16,16,128]{3,2,1,0:T(8,128)(2,1)S(1)}, u32[]{:S(2)}, u32[]{:S(2)}) collective-permute-start(bf16[1,16,16,128]{3,2,1,0:T(8,128)(2,1)S(1)} %get-tuple-element.118), channel_id=1, source_target_pairs={{0,1},{1,2},{2,3},{3,4},{4,5},{5,6},{6,7},{7,8},{8,9},{9,10},{10,1... | collective-permute-start | bytes 196616 | tf_op jit(solution)/shard_map/ppermute | solution.py:293
  24.5 11.8 %collective-permute-start.4 = (bf16[1,16,16,128]{3,2,1,0:T(8,128)(2,1)S(1)}, bf16[1,16,16,128]{3,2,1,0:T(8,128)(2,1)S(1)}, u32[]{:S(2)}, u32[]{:S(2)}) collective-permute-start(bf16[1,16,16,128]{3,2,1,0:T(8,128)(2,1)S(1)} %get-tuple-element.117), channel_id=1, source_target_pairs={{1,0},{2,1},{3,2},{4,3},{5,4},{6,5},{7,6},{8,7},{9,8},{10,9},{11,1... | collective-permute-start | bytes 196616 | tf_op jit(solution)/shard_map/ppermute | solution.py:294
  43.4 14.0 %copy-start.3 = (bf16[1,2,27,128,128]{4,3,2,1,0:T(8,128)(2,1)S(1)}, bf16[1,2,27,128,128]{4,3,2,1,0:T(8,128)(2,1)}, u32[]{:S(2)}) copy-start(bf16[1,2,27,128,128]{4,3,2,1,0:T(8,128)(2,1)} %w_g.3) | copy-start | bytes 5308420
  43.4 4.4 %collective-permute-start.6 = (bf16[4,2,27,16,128]{4,3,2,1,0:T(8,128)(2,1)}, bf16[4,2,27,16,128]{4,3,2,1,0:T(8,128)(2,1)}, u32[]{:S(2)}, u32[]{:S(2)}) collective-permute-start(bf16[4,2,27,16,128]{4,3,2,1,0:T(8,128)(2,1)} %get-tuple-element.79), channel_id=1, source_target_pairs={{0,1},{1,0},{2,3},{3,2},{4,5},{5,4},{6,7},{7,6},{8,9},{9,8},{10,11... | collective-permute-start | bytes 2654216 | tf_op jit(solution)/shard_map/ppermute | solution.py:307
  43.5 5.8 %copy-start.7 = (bf16[1,6,16,16,256]{4,3,2,1,0:T(8,128)(2,1)S(1)}, bf16[1,6,16,16,256]{4,3,2,1,0:T(8,128)(2,1)}, u32[]{:S(2)}) copy-start(bf16[1,6,16,16,256]{4,3,2,1,0:T(8,128)(2,1)} %param.5) | copy-start | bytes 2359300
  43.5 8.2 %collective-permute-start.8 = (bf16[1,16,16,128]{3,2,1,0:T(8,128)(2,1)S(1)}, bf16[1,16,16,128]{3,2,1,0:T(8,128)(2,1)S(1)}, u32[]{:S(2)}, u32[]{:S(2)}) collective-permute-start(bf16[1,16,16,128]{3,2,1,0:T(8,128)(2,1)S(1)} %get-tuple-element.116), channel_id=1, source_target_pairs={{0,1},{1,2},{2,3},{3,4},{4,5},{5,6},{6,7},{7,8},{8,9},{9,10},{10,1... | collective-permute-start | bytes 196616 | tf_op jit(solution)/shard_map/ppermute | solution.py:293
  44.1 7.6 %collective-permute-start.9 = (bf16[1,16,16,128]{3,2,1,0:T(8,128)(2,1)S(1)}, bf16[1,16,16,128]{3,2,1,0:T(8,128)(2,1)S(1)}, u32[]{:S(2)}, u32[]{:S(2)}) collective-permute-start(bf16[1,16,16,128]{3,2,1,0:T(8,128)(2,1)S(1)} %get-tuple-element.115), channel_id=1, source_target_pairs={{1,0},{2,1},{3,2},{4,3},{5,4},{6,5},{7,6},{8,7},{9,8},{10,9},{11,1... | collective-permute-start | bytes 196616 | tf_op jit(solution)/shard_map/ppermute | solution.py:294
  49.2 8.0 %collective-permute-start.7 = (bf16[2,27,16,128]{3,2,1,0:T(8,128)(2,1)S(1)}, bf16[2,27,16,128]{3,2,1,0:T(8,128)(2,1)S(1)}, u32[]{:S(2)}, u32[]{:S(2)}) collective-permute-start(bf16[2,27,16,128]{3,2,1,0:T(8,128)(2,1)S(1)} %get-tuple-element.112), channel_id=1, source_target_pairs={{0,4},{1,29},{2,6},{3,31},{4,8},{5,1},{6,10},{7,3},{8,12},{9,5},{1... | collective-permute-start | bytes 663560 | tf_op jit(solution)/shard_map/ppermute | solution.py:307
  49.3 21.2 %collective-permute-start.12 = (bf16[6,16,16,256]{3,2,1,0:T(8,128)(2,1)S(1)}, bf16[6,16,16,256]{3,2,1,0:T(8,128)(2,1)S(1)}, u32[]{:S(2)}, u32[]{:S(2)}) collective-permute-start(bf16[6,16,16,256]{3,2,1,0:T(8,128)(2,1)S(1)} %bitcast.27), channel_id=1, source_target_pairs={{224,0},{0,32},{32,64},{64,96},{96,128},{128,160},{160,192},{192,2... | collective-permute-start | bytes 2359304 | tf_op jit(solution)/shard_map/ppermute | solution.py:288
  57.3 7.2 %collective-permute-start.10 = (bf16[2,27,16,128]{3,2,1,0:T(8,128)(2,1)S(1)}, bf16[2,27,16,128]{3,2,1,0:T(8,128)(2,1)S(1)}, u32[]{:S(2)}, u32[]{:S(2)}) collective-permute-start(bf16[2,27,16,128]{3,2,1,0:T(8,128)(2,1)S(1)} %add_convert_fusion.4), channel_id=1, source_target_pairs={{0,4},{1,29},{2,6},{3,31},{4,8},{5,1},{6,10},{7,3},{8,12},{9,5},{1... | collective-permute-start | bytes 663560 | tf_op jit(solution)/shard_map/ppermute | solution.py:307
  64.6 7.2 %collective-permute-start.11 = (bf16[2,27,16,128]{3,2,1,0:T(8,128)(2,1)S(1)}, bf16[2,27,16,128]{3,2,1,0:T(8,128)(2,1)S(1)}, u32[]{:S(2)}, u32[]{:S(2)}) collective-permute-start(bf16[2,27,16,128]{3,2,1,0:T(8,128)(2,1)S(1)} %add_convert_fusion.3), channel_id=1, source_target_pairs={{0,4},{1,29},{2,6},{3,31},{4,8},{5,1},{6,10},{7,3},{8,12},{9,5},{1... | collective-permute-start | bytes 663560 | tf_op jit(solution)/shard_map/ppermute | solution.py:307
  71.9 9.3 %collective-permute-start.14 = (bf16[2,27,16,128]{3,2,1,0:T(8,128)(2,1)S(1)}, bf16[2,27,16,128]{3,2,1,0:T(8,128)(2,1)S(1)}, u32[]{:S(2)}, u32[]{:S(2)}) collective-permute-start(bf16[2,27,16,128]{3,2,1,0:T(8,128)(2,1)S(1)} %add_convert_fusion.2), channel_id=1, source_target_pairs={{0,6},{1,3},{2,4},{3,1},{4,10},{5,7},{6,8},{7,5},{8,14},{9,11},{10... | collective-permute-start | bytes 663560 | tf_op jit(solution)/shard_map/ppermute | solution.py:307
  74.2 11.8 %collective-permute-start.13 = (bf16[2,27,16,128]{3,2,1,0:T(8,128)(2,1)S(1)}, bf16[2,27,16,128]{3,2,1,0:T(8,128)(2,1)S(1)}, u32[]{:S(2)}, u32[]{:S(2)}) collective-permute-start(bf16[2,27,16,128]{3,2,1,0:T(8,128)(2,1)S(1)} %add_convert_fusion.2), channel_id=1, source_target_pairs={{0,4},{1,1},{2,6},{3,3},{4,8},{5,5},{6,10},{7,7},{8,12},{9,9},{10,... | collective-permute-start | bytes 663560 | tf_op jit(solution)/shard_map/ppermute | solution.py:307
  86.0 2.0 %collective-permute-start.15 = (bf16[2,27,16,128]{3,2,1,0:T(8,128)(2,1)S(1)}, bf16[2,27,16,128]{3,2,1,0:T(8,128)(2,1)S(1)}, u32[]{:S(2)}, u32[]{:S(2)}) collective-permute-start(bf16[2,27,16,128]{3,2,1,0:T(8,128)(2,1)S(1)} %add_convert_fusion.1), channel_id=1, source_target_pairs={{0,1},{1,0},{2,3},{3,2},{4,5},{5,4},{6,7},{7,6},{8,9},{9,8},{10,11... | collective-permute-start | bytes 663560 | tf_op jit(solution)/shard_map/ppermute | solution.py:307
  86.2 7.0 %collective-permute-start.17 = (bf16[2,16,16,256]{3,2,1,0:T(8,128)(2,1)S(1)}, bf16[2,16,16,256]{3,2,1,0:T(8,128)(2,1)S(1)}, u32[]{:S(2)}, u32[]{:S(2)}) collective-permute-start(bf16[2,16,16,256]{3,2,1,0:T(8,128)(2,1)S(1)} %get-tuple-element.114), channel_id=1, source_target_pairs={{0,1},{1,2},{2,3},{3,4},{4,5},{5,6},{6,7},{7,8},{8,9},{9,10},{10,1... | collective-permute-start | bytes 786440 | tf_op jit(solution)/shard_map/ppermute | solution.py:293
  86.8 7.8 %collective-permute-start.18 = (bf16[2,16,16,256]{3,2,1,0:T(8,128)(2,1)S(1)}, bf16[2,16,16,256]{3,2,1,0:T(8,128)(2,1)S(1)}, u32[]{:S(2)}, u32[]{:S(2)}) collective-permute-start(bf16[2,16,16,256]{3,2,1,0:T(8,128)(2,1)S(1)} %get-tuple-element.113), channel_id=1, source_target_pairs={{1,0},{2,1},{3,2},{4,3},{5,4},{6,5},{7,6},{8,7},{9,8},{10,9},{11,1... | collective-permute-start | bytes 786440 | tf_op jit(solution)/shard_map/ppermute | solution.py:294
  88.1 7.2 %collective-permute-start.16 = (bf16[2,27,16,128]{3,2,1,0:T(8,128)(2,1)S(1)}, bf16[2,27,16,128]{3,2,1,0:T(8,128)(2,1)S(1)}, u32[]{:S(2)}, u32[]{:S(2)}) collective-permute-start(bf16[2,27,16,128]{3,2,1,0:T(8,128)(2,1)S(1)} %add_convert_fusion.refs_0_), channel_id=1, source_target_pairs={{0,4},{1,29},{2,6},{3,31},{4,8},{5,1},{6,10},{7,3},{8,12},{9,5},{1... | collective-permute-start | bytes 663560 | tf_op jit(solution)/shard_map/ppermute | solution.py:307
  95.3 8.1 %collective-permute-start.19 = (bf16[2,27,16,128]{3,2,1,0:T(8,128)(2,1)S(1)}, bf16[2,27,16,128]{3,2,1,0:T(8,128)(2,1)S(1)}, u32[]{:S(2)}, u32[]{:S(2)}) collective-permute-start(bf16[2,27,16,128]{3,2,1,0:T(8,128)(2,1)S(1)} %collective-permute-done.16.refs_1_), channel_id=1, source_target_pairs={{0,4},{1,29},{2,6},{3,31},{4,8},{5,1},{6,10},{7,3},{8,12},{9,5},{1... | collective-permute-start | bytes 663560 | tf_op jit(solution)/shard_map/ppermute | solution.py:307
  95.3 8.1 %collective-permute-start.20 = (bf16[2,27,16,128]{3,2,1,0:T(8,128)(2,1)S(1)}, bf16[2,27,16,128]{3,2,1,0:T(8,128)(2,1)S(1)}, u32[]{:S(2)}, u32[]{:S(2)}) collective-permute-start(bf16[2,27,16,128]{3,2,1,0:T(8,128)(2,1)S(1)} %collective-permute-done.16.refs_1_), channel_id=1, source_target_pairs={{0,1},{1,0},{2,3},{3,2},{4,5},{5,4},{6,7},{7,6},{8,9},{9,8},{10,11... | collective-permute-start | bytes 663560 | tf_op jit(solution)/shard_map/ppermute | solution.py:307
  103.4 8.4 %copy-start = (f32[1,2,27,128,128]{4,3,2,1,0:T(8,128)S(1)}, f32[1,2,27,128,128]{4,3,2,1,0:T(8,128)}, u32[]{:S(2)}) copy-start(f32[1,2,27,128,128]{4,3,2,1,0:T(8,128)} %momentum.3) | copy-start | bytes 10616836
  103.4 7.2 %collective-permute-start.21 = (bf16[2,27,16,128]{3,2,1,0:T(8,128)(2,1)S(1)}, bf16[2,27,16,128]{3,2,1,0:T(8,128)(2,1)S(1)}, u32[]{:S(2)}, u32[]{:S(2)}) collective-permute-start(bf16[2,27,16,128]{3,2,1,0:T(8,128)(2,1)S(1)} %collective-permute-done.19.refs_3_), channel_id=1, source_target_pairs={{0,4},{1,29},{2,6},{3,31},{4,8},{5,1},{6,10},{7,3},{8,12},{9,5},{1... | collective-permute-start | bytes 663560 | tf_op jit(solution)/shard_map/ppermute | solution.py:307
  103.5 7.1 %collective-permute-start.22 = (bf16[2,27,16,128]{3,2,1,0:T(8,128)(2,1)S(1)}, bf16[2,27,16,128]{3,2,1,0:T(8,128)(2,1)S(1)}, u32[]{:S(2)}, u32[]{:S(2)}) collective-permute-start(bf16[2,27,16,128]{3,2,1,0:T(8,128)(2,1)S(1)} %collective-permute-done.19.refs_3_), channel_id=1, source_target_pairs={{0,1},{1,0},{2,3},{3,2},{4,5},{5,4},{6,7},{7,6},{8,9},{9,8},{10,11... | collective-permute-start | bytes 663560 | tf_op jit(solution)/shard_map/ppermute | solution.py:307
  110.7 7.1 %collective-permute-start.23 = (bf16[2,27,16,128]{3,2,1,0:T(8,128)(2,1)S(1)}, bf16[2,27,16,128]{3,2,1,0:T(8,128)(2,1)S(1)}, u32[]{:S(2)}, u32[]{:S(2)}) collective-permute-start(bf16[2,27,16,128]{3,2,1,0:T(8,128)(2,1)S(1)} %collective-permute-done.21.refs_0_), channel_id=1, source_target_pairs={{0,4},{1,29},{2,6},{3,31},{4,8},{5,1},{6,10},{7,3},{8,12},{9,5},{1... | collective-permute-start | bytes 663560 | tf_op jit(solution)/shard_map/ppermute | solution.py:307
  110.7 7.1 %collective-permute-start.24 = (bf16[2,27,16,128]{3,2,1,0:T(8,128)(2,1)S(1)}, bf16[2,27,16,128]{3,2,1,0:T(8,128)(2,1)S(1)}, u32[]{:S(2)}, u32[]{:S(2)}) collective-permute-start(bf16[2,27,16,128]{3,2,1,0:T(8,128)(2,1)S(1)} %collective-permute-done.21.refs_0_), channel_id=1, source_target_pairs={{0,1},{1,0},{2,3},{3,2},{4,5},{5,4},{6,7},{7,6},{8,9},{9,8},{10,11... | collective-permute-start | bytes 663560 | tf_op jit(solution)/shard_map/ppermute | solution.py:307
  (1 other events, 1.1 us)
